TPU v7x, 128 devices: a whole 4x4x4 slice. The times are simulated.
128 devices in a mesh: row: 16 (over y, x), col: 8 (over z, core).
Axes of the slice: x: 4, y: 4, z: 4, core: 2. Of those that a mesh axis runs over, the one named last changes fastest.
Arguments:
- elevation: float32 [16384, 16384], P('row', 'col'), may hold values from -12 to 12
- source_row: int32 [2048, 1], P(('row', 'col')), may hold values from 0 to 15, as said below
- source_block: int32 [2048, 1], P(('row', 'col')), may hold values from 0 to 31, as said below
- row_weights: bfloat16 [2048, 256, 256], P(('row', 'col')), may hold values from 0 to 1, as said below
- col_weights: bfloat16 [2048, 256, 256], P(('row', 'col')), may hold values from 0 to 1, as said below
Outputs:
- mercator: float32 [8192, 16384], P('row', 'col')
- overview_one: float32 [4096, 8192], P('row', 'col')
- overview_two: float32 [16, 8, 256, 256], P('row', 'col')
Inputs may be any that keep to these rules, and one draw needn't show every extreme that they name: source_row[t] differs from the row index of t's own device by at most one; the targets of one device that share a tile row name the same value. The targets of one device that share a tile row name the same block row, source_block // 8; the block column source_block % (8) differs by at most one from (j % 8) (8) // 8, where j is the target's slot on its device. `row_weights`: entry (t, i, k) is zero unless k is (254) i // 255 or one more; those two entries lie in [0, 1] and sum to one up to bfloat16 rounding. `col_weights`: entry (t, k, l) is zero unless k is (254) l // 255 or one more; those two entries lie in [0, 1] and sum to one up to bfloat16 rounding.
All inputs are finite; a program needn't handle non-finite values.
Results may differ from a plain program's by a relative error of at most 0.0033.
Values may be sent and summed in bfloat16 or wider, within the bound.
A program may use at most 512 MiB of HBM per device.

v0:
```python
import math

import jax
import jax.numpy as jnp
from jax import lax
from jax.sharding import PartitionSpec as P

B = 256
TR_DEV = 2
TC_DEV = 8


SUN_COS = math.cos(math.pi / 4.0)
SUN_SIN = math.sin(math.pi / 4.0)
AZIMUTH_ANGLES = (1.25 * math.pi, 1.5 * math.pi, 1.75 * math.pi, 2.0 * math.pi)


def with_halo(cells, sides, width):
    for axis, dim in sides:
        count = lax.axis_size(axis)
        ends = count - 1
        head = lax.slice_in_dim(cells, 0, width, axis=dim)
        tail = lax.slice_in_dim(cells, cells.shape[dim] - width, cells.shape[dim], axis=dim)
        cells = jnp.concatenate(
            [
                lax.ppermute(tail, axis, [(i, (i + 1) % count) for i in range(ends)]),
                cells,
                lax.ppermute(head, axis, [((i + 1) % count, i) for i in range(ends)]),
            ],
            axis=dim,
        )
    return cells


def swapped(array, axis, distance):
    return lax.ppermute(array, axis, [(i, i ^ 1 << distance) for i in range(lax.axis_size(axis))])


def shade(padded):
    upper_left = padded[..., :-2, :-2]
    upper_mid = padded[..., :-2, 1:-1]
    upper_right = padded[..., :-2, 2:]
    middle_left = padded[..., 1:-1, :-2]
    middle_right = padded[..., 1:-1, 2:]
    lower_left = padded[..., 2:, :-2]
    lower_mid = padded[..., 2:, 1:-1]
    lower_right = padded[..., 2:, 2:]
    east_slope = (
        upper_right
        + 2.0 * middle_right
        + lower_right
        - (upper_left + 2.0 * middle_left + lower_left)
    ) * 0.125
    south_slope = (
        lower_left + 2.0 * lower_mid + lower_right - (upper_left + 2.0 * upper_mid + upper_right)
    ) * 0.125
    scale_back = 1.0 / jnp.sqrt(1.0 + east_slope * east_slope + south_slope * south_slope)
    lit_total = jnp.zeros_like(east_slope)
    for azimuth in AZIMUTH_ANGLES:
        along_light = east_slope * math.sin(azimuth) - south_slope * math.cos(azimuth)
        lit_total = lit_total + jnp.maximum(SUN_COS - SUN_SIN * along_light, 0.0)
    return 0.25 * lit_total * scale_back


def halve_image(picture):
    pic_rows, pic_cols = picture.shape
    return jnp.sum(picture.reshape(pic_rows // 2, 2, pic_cols // 2, 2), axis=(1, 3)) * 0.25


def rim_padded(elevation):
    return with_halo(elevation, (("row", 0), ("col", 1)), 1)


def cut_blocks(source, wanted, block_cols, extent):
    valid = wanted >= 0
    index = jnp.maximum(wanted, 0)
    start_rows = index // block_cols * B
    start_cols = index % block_cols * B

    def cut_one(row_start, col_start):
        return lax.dynamic_slice(source, (row_start, col_start), (extent, extent))

    pieces = jax.vmap(cut_one)(start_rows, start_cols)
    return jnp.where(valid[..., None, None], pieces, jnp.zeros((), source.dtype))


def choose_blocks(offset, from_above, from_below, from_here):
    above_mask = (offset < 0)[:, None, None]
    below_mask = (offset > 0)[:, None, None]
    return jnp.where(above_mask, from_above, jnp.where(below_mask, from_below, from_here))


def per_device(elevation, source_row, source_block, row_weights, col_weights):
    rows_local, cols_local = elevation.shape
    block_cols = cols_local // B
    sources = source_row[:, 0]
    numbers = source_block[:, 0]
    offset = sources - lax.axis_index("row")
    want_above = jnp.where(offset < 0, numbers, -1)
    want_below = jnp.where(offset > 0, numbers, -1)
    want_here = jnp.where(offset == 0, numbers, -1)
    asked = with_halo(jnp.stack([want_above, want_below]), (("row", 0),), 1)
    for_above = asked[0]
    for_below = asked[3]
    padded = rim_padded(elevation)
    answers = jnp.stack(
        [
            cut_blocks(padded, for_above, block_cols, B + 2),
            cut_blocks(padded, for_below, block_cols, B + 2),
        ]
    )
    returned = with_halo(answers, (("row", 0),), 1)
    rimmed = choose_blocks(
        offset, returned[0], returned[3], cut_blocks(padded, want_here, block_cols, B + 2)
    )
    picked = shade(rimmed).astype(jnp.bfloat16)
    inner_rows = jnp.einsum(
        "tik,tkl->til", row_weights, picked, preferred_element_type=jnp.float32
    ).astype(jnp.bfloat16)
    mercator = jnp.einsum(
        "rcik,rckl->ricl",
        inner_rows.reshape(TR_DEV, TC_DEV, B, B),
        col_weights.reshape(TR_DEV, TC_DEV, B, B),
        preferred_element_type=jnp.float32,
    ).reshape(TR_DEV * B, TC_DEV * B)
    overview_one = halve_image(mercator)
    level_two = halve_image(overview_one)
    parity = lax.axis_index("row") % 2
    own_half = lax.dynamic_slice_in_dim(level_two, parity * B, B, 1)
    other_half = lax.dynamic_slice_in_dim(level_two, (1 - parity) * B, B, 1)
    partner_half = swapped(other_half, "row", 0)
    coarse_tile = jnp.where(
        parity == 0,
        jnp.concatenate([own_half, partner_half], axis=0),
        jnp.concatenate([partner_half, own_half], axis=0),
    )
    return (mercator, overview_one, coarse_tile.reshape(1, 1, B, B))


def solution(mesh):
    in_specs = (
        P("row", "col"),
        P(("row", "col"), None),
        P(("row", "col"), None),
        P(("row", "col"), None, None),
        P(("row", "col"), None, None),
    )
    out_specs = (P("row", "col"), P("row", "col"), P("row", "col", None, None))
    return jax.shard_map(
        per_device, mesh=mesh, in_specs=in_specs, out_specs=out_specs, check_vma=False
    )
```

profile of v0, /device:TPU:0, one launch (start us, length us, event | category | flops | bytes accessed | tf_op | source)
XLA Modules:
  0.0 1217.6 jit_solution(8698462690660486599)
XLA Ops:
  24.9 11.5 concatenate.39
  43.7 25.9 %concatenate.40 = f32[1026,2050]{0,1:T(8,128)} concatenate(f32[1026,1]{0,1:T(1,128)S(1)} %collective-permute-done.3, f32[1026,2048]{0,1:T(8,128)} %concatenate.39, f32[1026,1]{0,1:T(1,128)S(1)} %collective-permute-done.4), dimensions={1} | concatenate | bytes 16826400 | tf_op jit(solution)/shard_map/concatenate | solution.py:24
  69.6 11.8 copy.33
  84.5 205.3 %while.3 = (s32[]{:T(128)}, f32[1026,2050]{1,0:T(8,128)}, s32[16,2]{0,1:T(2,128)S(1)}, f32[16,258,258]{2,0,1:T(8,128)}, s32[]{:T(128)}, /*index=5*/s32[]{:T(128)}) while((s32[]{:T(128)}, f32[1026,2050]{1,0:T(8,128)}, s32[16,2]{0,1:T(2,128)S(1)}, f32[16,258,258]{2,0,1:T(8,128)}, s32[]{:T(128)}, /*index=5*/s32[]{:T(128)}) %tuple.73), condition=%wide.while_cond, body=%wide.while_body.sunk | while | flops 2 | bytes 1597653 | solution.py:81
  306.0 205.7 %while.4 = (s32[]{:T(128)}, f32[1026,2050]{1,0:T(8,128)}, s32[16,2]{0,1:T(2,128)S(1)}, f32[16,258,258]{2,0,1:T(8,128)}, s32[]{:T(128)}, /*index=5*/s32[]{:T(128)}) while((s32[]{:T(128)}, f32[1026,2050]{1,0:T(8,128)}, s32[16,2]{0,1:T(2,128)S(1)}, f32[16,258,258]{2,0,1:T(8,128)}, s32[]{:T(128)}, /*index=5*/s32[]{:T(128)}) %tuple.79), condition=%wide.while_cond.1, body=%wide.while_body.1.sunk | while | flops 2 | bytes 1597653 | solution.py:81
  309.5 9.3 dynamic-update-slice.10
  322.4 9.3 dynamic-update-slice.10
  335.3 9.3 dynamic-update-slice.10
  348.1 9.3 dynamic-update-slice.10
  361.0 9.3 dynamic-update-slice.10
  373.8 9.3 dynamic-update-slice.10
  386.7 9.3 dynamic-update-slice.10
  399.5 9.3 dynamic-update-slice.10
  522.0 205.4 %while.5 = (s32[]{:T(128)}, f32[1026,2050]{1,0:T(8,128)}, s32[16,2]{0,1:T(2,128)S(1)}, f32[16,258,258]{2,0,1:T(8,128)}, s32[]{:T(128)}, /*index=5*/s32[]{:T(128)}) while((s32[]{:T(128)}, f32[1026,2050]{1,0:T(8,128)}, s32[16,2]{0,1:T(2,128)S(1)}, f32[16,258,258]{2,0,1:T(8,128)}, s32[]{:T(128)}, /*index=5*/s32[]{:T(128)}) %tuple.80), condition=%wide.while_cond.2, body=%wide.while_body.2.sunk | while | flops 2 | bytes 1597653 | solution.py:81
  628.1 9.3 dynamic-update-slice.11
  641.0 9.3 dynamic-update-slice.11
  653.8 9.3 dynamic-update-slice.11
  679.5 9.3 dynamic-update-slice.11
  727.4 10.4 fusion
  737.9 22.8 %multiply_convert_fusion = bf16[16,256,256]{2,0,1:T(8,128)(2,1)S(1)} fusion(f32[16,258,258]{2,0,1:T(8,128)} %fusion), kind=kLoop, calls=%fused_computation.24 | loop fusion | flops 50331648 | bytes 35651584 | tf_op jit(solution)/shard_map/convert_element_type | solution.py:116
  767.3 270.3 %reshape_reshape.3 = f32[256,2,1024,2]{3,2,1,0:T(8,128)} reshape(f32[2,256,8,256]{3,2,1,0:T(8,128)} %copy.44) | data formatting | bytes 8388608 | tf_op jit(solution)/shard_map/reshape;reshape | solution.py:67
  1037.7 80.5 %reduce_sum.18 = f32[256,1024]{1,0:T(8,128)S(1)} reduce(f32[256,2,1024,2]{3,2,1,0:T(8,128)} %reshape_reshape.3, f32[]{:T(128)} %constant.109.clone.1), dimensions={1,3}, to_apply=%region_0.1 | reduce | flops 786432 | bytes 5242884 | tf_op jit(solution)/shard_map/reduce_sum | solution.py:67
  1118.3 68.6 %mul.181 = f32[128,2,512,2]{3,2,1,0:T(8,128)} reshape(f32[256,1024]{1,0:T(8,128)S(1)} %broadcast_multiply_fusion) | data formatting | bytes 2097152 | tf_op jit(solution)/shard_map/mul | solution.py:67
  1186.8 21.1 %reduce_sum.19 = f32[128,512]{1,0:T(8,128)S(1)} reduce(f32[128,2,512,2]{3,2,1,0:T(8,128)} %mul.181, f32[]{:T(128)} %constant.109.clone.1), dimensions={1,3}, to_apply=%region_1.2 | reduce | flops 196608 | bytes 1310724 | tf_op jit(solution)/shard_map/reduce_sum | solution.py:67
  (282 shorter events, 581.5 us)
Async XLA Ops:
  0.6 761.5 %copy-start = (bf16[16,256,256]{2,1,0:T(8,128)(2,1)S(1)}, bf16[16,256,256]{2,1,0:T(8,128)(2,1)}, u32[]{:S(2)}) copy-start(bf16[16,256,256]{2,1,0:T(8,128)(2,1)} %param.9) | copy-start | bytes 6291460
  2.1 20.9 %collective-permute-start = (s32[1,16]{1,0:T(1,128)S(1)}, s32[1,16]{1,0:T(1,128)S(1)}, u32[]{:S(2)}, u32[]{:S(2)}) collective-permute-start(s32[1,16]{1,0:T(1,128)S(1)} %get-tuple-element.91), channel_id=1, source_target_pairs={{8,0},{16,8},{24,16},{32,24},{40,32},{48,40},{56,48},{64,56},{72,6... | collective-permute-start | bytes 200 | tf_op jit(solution)/shard_map/ppermute | solution.py:28
  3.4 19.7 %collective-permute-start.6 = (s32[1,16]{1,0:T(1,128)S(1)}, s32[1,16]{1,0:T(1,128)S(1)}, u32[]{:S(2)}, u32[]{:S(2)}) collective-permute-start(s32[1,16]{1,0:T(1,128)S(1)} %get-tuple-element.92), channel_id=1, source_target_pairs={{0,8},{8,16},{16,24},{24,32},{32,40},{40,48},{48,56},{56,64},{64,7... | collective-permute-start | bytes 200 | tf_op jit(solution)/shard_map/ppermute | solution.py:26
  8.9 14.3 %collective-permute-start.1 = (f32[1,2048]{1,0:T(1,128)S(1)}, f32[1,2048]{1,0:T(1,128)S(1)}, u32[]{:S(2)}, u32[]{:S(2)}) collective-permute-start(f32[1,2048]{1,0:T(1,128)S(1)} %get-tuple-element.86), channel_id=1, source_target_pairs={{0,8},{8,16},{16,24},{24,32},{32,40},{40,48},{48,56},{56,64},{64,7... | collective-permute-start | bytes 24584 | tf_op jit(solution)/shard_map/ppermute | solution.py:26
  12.4 10.6 copy-start.4
  12.4 11.1 collective-permute-start.2
  37.2 2.6 collective-permute-start.3
  38.5 5.2 collective-permute-start.4
  295.7 431.8 %collective-permute-start.5 = (f32[1,16,258,258]{3,1,2,0:T(8,128)}, f32[1,16,258,258]{3,1,2,0:T(8,128)}, u32[]{:S(2)}, u32[]{:S(2)}) collective-permute-start(f32[1,16,258,258]{3,1,2,0:T(8,128)} %bitcast_select_fusion.2), channel_id=1, source_target_pairs={{0,8},{8,16},{16,24},{24,32},{32,40},{40,48},{48,56},{56,64},{64,7... | collective-permute-start | bytes 12780296 | tf_op jit(solution)/shard_map/ppermute | solution.py:26
  517.7 209.7 %collective-permute-start.7 = (f32[1,16,258,258]{3,1,2,0:T(8,128)}, f32[1,16,258,258]{3,1,2,0:T(8,128)}, u32[]{:S(2)}, u32[]{:S(2)}) collective-permute-start(f32[1,16,258,258]{3,1,2,0:T(8,128)} %bitcast_select_fusion.1), channel_id=1, source_target_pairs={{8,0},{16,8},{24,16},{32,24},{40,32},{48,40},{56,48},{64,56},{72,6... | collective-permute-start | bytes 12780296 | tf_op jit(solution)/shard_map/ppermute | solution.py:28
  737.9 22.8 %copy-start.3 = (bf16[16,256,256]{2,1,0:T(8,128)(2,1)S(1)}, bf16[16,256,256]{2,1,0:T(8,128)(2,1)}, u32[]{:S(2)}) copy-start(bf16[16,256,256]{2,1,0:T(8,128)(2,1)} %param.8) | copy-start | bytes 6291460
  1118.3 68.6 %copy-start.2 = (f32[256,1024]{1,0:T(8,128)}, f32[256,1024]{1,0:T(8,128)S(1)}, u32[]{:S(2)}) copy-start(f32[256,1024]{1,0:T(8,128)S(1)} %broadcast_multiply_fusion) | copy-start | bytes 3145732
  1208.0 8.9 collective-permute-start.8
  1210.6 7.0 copy-start.1
where the time goes:
time: 1240 us; the launch traced here: 1220 us
  local copies, waits for them, and re-layouts  1040 us (84%)
  other arithmetic  149 us (12%)
  starting transfers between devices  24.3 us (2%)
    gather x240, local copies, waits for them, and re-layouts  616 us
    another operation x1, local copies, waits for them, and re-layouts, halve_image(): picture.reshape(pic_rows // 2, 2, pic_cols // 2, 2)  270 us
    reduce_sum x2, other arithmetic, halve_image(): jnp.sum(picture.reshape(pic_rows // 2, 2, pic_cols // 2, 2), axis=(1, 3))  102 us
    mul x1, local copies, waits for them, and re-layouts, halve_image(): jnp.sum(picture.reshape(pic_rows // 2, 2, pic_cols // 2, 2), axis=(1, 3))  68.6 us
    concatenate x2, local copies, waits for them, and re-layouts, with_halo(): jnp.concatenate([lax.ppermute(tail, axis, [(i, (i + 1) % count) for i in...  37.4 us
    unnamed x16, local copies, waits for them, and re-layouts  36.7 us
  transfers between devices with their start and end apart: 9, of which 1 were waited for; matrix products, arithmetic and copies ran while one was open for 36% of the time, Pallas kernels for 0%

commit v1 on v0

v1 whole, which is shorter than its diff:
```python
import functools
import math

import jax
import jax.numpy as jnp
from jax import lax
from jax.experimental import pallas as pl
from jax.experimental.pallas import tpu as pltpu
from jax.sharding import PartitionSpec as P

B = 256
HALF = B // 2
TR_DEV = 2
TC_DEV = 8
PAD_R = 8
PAD_C = 128
BAND = 32
ORDER = (1, 2, 3, 4, 0, 5, 6, 7)
READY = ((), (), (2,), (3,), (0, 1), (4,), (5,), (6, 7))

SUN_COS = math.cos(math.pi / 4.0)
MESH = pl.DeviceIdType.MESH


def lit_of(east, south):
    base = 0.25 * SUN_COS
    straight = base / 8.0
    slanted = 0.25 * 0.5 / 8.0
    scale = lax.rsqrt(1.0 + (east * east + south * south) * (1.0 / 64.0))
    lit = jnp.maximum(base + (east - south) * slanted, 0.0)
    lit = lit + jnp.maximum(base + east * straight, 0.0)
    lit = lit + jnp.maximum(base + (east + south) * slanted, 0.0)
    lit = lit + jnp.maximum(base + south * straight, 0.0)
    return lit * scale


def chosen(index, options):
    value = options[0]
    for k, option in enumerate(options[1:], 1):
        value = jnp.where(index == k, option, value)
    return value


def pooled(both, pool):
    high = both.astype(jnp.bfloat16)
    low = (both - high.astype(jnp.float32)).astype(jnp.bfloat16)
    return jnp.dot(high, pool, preferred_element_type=jnp.float32) + jnp.dot(
        low, pool, preferred_element_type=jnp.float32
    )


def kernel(
    n_row, n_col,
    ask_ref, ask_hbm, elev_hbm, roww_hbm, colw_hbm,
    merc_hbm, one_hbm, two_hbm,
    padded, shaded, asked, asked_s, sendbuf, merged, roww, colw, tiles, ones, two_own, two_send, two_got,
    *rest,
):
    recv = rest[:16]
    (load_sem, ask_send, ask_recv, ask_local, halo_send, halo_recv,
     strip_send, strip_recv, two_sems, out_sem) = rest[16:]
    row = lax.axis_index("row")
    col = lax.axis_index("col")
    rows, cols = elev_hbm.shape
    parity = lax.rem(row, 2)
    up = lax.rem(row + n_row - 1, n_row)
    down = lax.rem(row + 1, n_row)
    left = lax.rem(col + n_col - 1, n_col)
    right = lax.rem(col + 1, n_col)
    last = TC_DEV - 1

    def sent_col(m):
        return m + parity * (last - 2 * m)

    def got_col(m):
        return (last - m) + parity * (2 * m - last)

    inner = padded.at[pl.ds(PAD_R, rows), pl.ds(PAD_C, cols)]
    load_elev = pltpu.make_async_copy(elev_hbm, inner, load_sem.at[0])
    load_elev.start()

    around = [(up, col), (down, col), (row, left), (row, right), (up, left), (up, right), (down, left), (down, right)]
    barrier = pltpu.get_barrier_semaphore()
    for device in around:
        pl.semaphore_signal(barrier, inc=1, device_id=device, device_id_type=MESH)
    pl.semaphore_wait(barrier, len(around))

    def remote(src, dst, send_sem, recv_sem, device):
        return pltpu.make_async_remote_copy(
            src_ref=src, dst_ref=dst, send_sem=send_sem, recv_sem=recv_sem, device_id=device, device_id_type=MESH
        )

    asks = [
        remote(ask_hbm, asked.at[1], ask_send.at[0], ask_recv.at[1], (up, col)),
        remote(ask_hbm, asked.at[0], ask_send.at[1], ask_recv.at[0], (down, col)),
    ]
    for copy in asks:
        copy.start()

    top, bottom = pl.ds(0, PAD_R), pl.ds(PAD_R + rows, PAD_R)
    mid_r, mid_c = pl.ds(PAD_R, rows), pl.ds(PAD_C, cols)
    west, east = pl.ds(0, PAD_C), pl.ds(PAD_C + cols, PAD_C)
    first_r, last_r = pl.ds(0, PAD_R), pl.ds(rows - PAD_R, PAD_R)
    first_c, last_c = pl.ds(0, PAD_C), pl.ds(cols - PAD_C, PAD_C)
    all_r, all_c = pl.ds(0, rows), pl.ds(0, cols)
    halo_plan = [
        ((first_r, all_c), (bottom, mid_c), (up, col)),
        ((last_r, all_c), (top, mid_c), (down, col)),
        ((all_r, first_c), (mid_r, east), (row, left)),
        ((all_r, last_c), (mid_r, west), (row, right)),
        ((first_r, first_c), (bottom, east), (up, left)),
        ((first_r, last_c), (bottom, west), (up, right)),
        ((last_r, first_c), (top, east), (down, left)),
        ((last_r, last_c), (top, west), (down, right)),
    ]
    halos = [
        remote(elev_hbm.at[src], padded.at[dst], halo_send.at[i], halo_recv.at[i], device)
        for i, (src, dst, device) in enumerate(halo_plan)
    ]
    for copy in halos:
        copy.start()
    load_roww = pltpu.make_async_copy(roww_hbm, roww, load_sem.at[1])
    load_colw = pltpu.make_async_copy(colw_hbm, colw, load_sem.at[2])
    load_roww.start()
    load_colw.start()

    for copy in asks:
        copy.wait_recv()
    to_scalar = pltpu.make_async_copy(asked, asked_s, ask_local)
    to_scalar.start()
    load_elev.wait()
    halos[0].wait_recv()
    halos[1].wait_recv()

    def clear(where):
        shape = tuple(s.size for s in where)
        padded[where] = jnp.zeros(shape, jnp.float32)

    @pl.when(row == 0)
    def _():
        clear((top, mid_c))

    @pl.when(row == n_row - 1)
    def _():
        clear((bottom, mid_c))

    to_scalar.wait()

    pool_rows = lax.broadcasted_iota(jnp.int32, (B, HALF), 0)
    pool_cols = lax.broadcasted_iota(jnp.int32, (B, HALF), 1)
    pool = jnp.where(pool_rows // 2 == pool_cols, 0.25, 0.0).astype(jnp.bfloat16)

    strips = []
    for step, m in enumerate(ORDER):
        if step == 4:
            for copy in halos[2:]:
                copy.wait_recv()

            @pl.when(col == 0)
            def _():
                clear((mid_r, west))

            @pl.when(col == n_col - 1)
            def _():
                clear((mid_r, east))

            @pl.when((row == 0) | (col == 0))
            def _():
                clear((top, west))

            @pl.when((row == 0) | (col == n_col - 1))
            def _():
                clear((top, east))

            @pl.when((row == n_row - 1) | (col == 0))
            def _():
                clear((bottom, west))

            @pl.when((row == n_row - 1) | (col == n_col - 1))
            def _():
                clear((bottom, east))

        lane = pl.multiple_of(sent_col(m) * B, PAD_C)
        slot = step % 2

        def shade_band(i, carry, lane=lane, slot=slot):
            start = pl.multiple_of(i * BAND, BAND)
            cells = padded[pl.ds(start, BAND + 2 * PAD_R), pl.ds(lane, B + 2 * PAD_C)]
            before = cells[:, PAD_C - 1 : PAD_C - 1 + B]
            here = cells[:, PAD_C : PAD_C + B]
            after = cells[:, PAD_C + 1 : PAD_C + 1 + B]
            across = after - before
            along = (before + after) + (here + here)
            middle = across[PAD_R : PAD_R + BAND]
            east8 = (across[PAD_R - 1 : PAD_R - 1 + BAND] + across[PAD_R + 1 : PAD_R + 1 + BAND]) + (middle + middle)
            south8 = along[PAD_R + 1 : PAD_R + 1 + BAND] - along[PAD_R - 1 : PAD_R - 1 + BAND]
            shaded[slot, pl.ds(start, BAND), :] = lit_of(east8, south8).astype(jnp.bfloat16)
            return carry

        lax.fori_loop(0, rows // BAND, shade_band, 0)
        for g in range(TR_DEV):
            for side in range(2):
                sendbuf[side, m, g] = chosen(
                    lax.div(asked_s[side, 1, g * TC_DEV], TC_DEV),
                    [shaded[slot, k * B : (k + 1) * B, :] for k in range(rows // B)],
                )
        for g in range(TR_DEV):
            for side, (device, place) in enumerate((((up, col), 2), ((down, col), 0))):
                copy = remote(
                    sendbuf.at[side, m, g],
                    recv[m * TR_DEV + g].at[place],
                    strip_send.at[side, m, g],
                    strip_recv.at[side, m, g],
                    device,
                )
                copy.start()
                strips.append(((step, g, side), copy))
        for g in range(TR_DEV):
            recv[(last - m) * TR_DEV + g][1] = chosen(
                lax.div(ask_ref[1, g * TC_DEV], TC_DEV),
                [shaded[slot, k * B : (k + 1) * B, :] for k in range(rows // B)],
            )
    strips = dict(strips)

    load_roww.wait()
    load_colw.wait()
    outs = []
    two_copy = remote(two_send, two_got, two_sems.at[0], two_sems.at[1], (row + 1 - 2 * parity, col))

    def out_copy(src, dst):
        copy = pltpu.make_async_copy(src, dst, out_sem.at[len(outs)])
        copy.start()
        outs.append(copy)

    def make_target(g, m):
        j = got_col(m)
        t = g * TC_DEV + j
        place = g * TC_DEV + m
        near = [k for k in (m - 1, m, m + 1) if 0 <= k <= last]
        wanted = lax.rem(ask_ref[1, t], TC_DEV)
        where = wanted + (1 - parity) * (last - 2 * wanted)
        source = chosen(where - near[0], [merged[g, k] for k in near])
        half_done = jnp.dot(roww[t], source, preferred_element_type=jnp.float32).astype(jnp.bfloat16)
        tile = jnp.dot(half_done, colw[t], preferred_element_type=jnp.float32)
        sums = []
        for half in range(2):
            tiles[place, half] = tile[:, half * HALF : (half + 1) * HALF]
            lane = pl.multiple_of(j * B + half * HALF, HALF)
            out_copy(tiles.at[place, half], merc_hbm.at[pl.ds(g * B, B), pl.ds(lane, HALF)])
            sums.append(tiles[place, half, pl.ds(0, HALF, stride=2), :] + tiles[place, half, pl.ds(1, HALF, stride=2), :])
        where = (g * 4 + m // 2, lax.rem(j, 2))
        ones[where] = pooled(jnp.concatenate(sums, axis=1), pool)
        lane = pl.multiple_of(j * HALF, HALF)
        out_copy(ones.at[where], one_hbm.at[pl.ds(g * HALF, HALF), pl.ds(lane, HALF)])

    def make_coarse(g, pair):
        actual = lax.div(got_col(2 * pair), 2)
        quarter = HALF // 2
        sums = [
            ones[g * 4 + pair, half, pl.ds(0, quarter, stride=2), :] + ones[g * 4 + pair, half, pl.ds(1, quarter, stride=2), :]
            for half in range(2)
        ]
        lane = pl.multiple_of(lax.rem(actual, 2) * HALF, HALF)
        dest = two_send if pair < 2 else two_own
        dest[pl.ds(g * quarter, quarter), pl.ds(lane, HALF)] = pooled(jnp.concatenate(sums, axis=1), pool)

    done = set()
    for step, m in enumerate(ORDER):
        for g in range(TR_DEV):
            strips[step, g, 0].wait_recv()
            strips[step, g, 1].wait_recv()
            side = ask_ref[0, g * TC_DEV] - row + 1
            merged[g, m] = chosen(side, [recv[m * TR_DEV + g][k] for k in range(3)])
            for target in READY[step]:
                make_target(g, target)
                done.add((g, target))
                pair = target // 2
                if (g, 2 * pair) in done and (g, 2 * pair + 1) in done:
                    make_coarse(g, pair)
        if step == 4:
            two_copy.start()
    out_copy(two_own, two_hbm.at[pl.ds(pl.multiple_of(parity * (HALF), HALF), HALF), :])
    two_copy.wait_recv()
    out_copy(two_got, two_hbm.at[pl.ds(pl.multiple_of((1 - parity) * (HALF), HALF), HALF), :])
    for copy in outs:
        copy.wait()
    two_copy.wait_send()
    for copy in asks + halos + list(strips.values()):
        copy.wait_send()


def per_device(n_row, n_col, elevation, source_row, source_block, row_weights, col_weights):
    rows, cols = elevation.shape
    targets = source_row.shape[0]
    ask = jnp.zeros((8, 128), jnp.int32)
    ask = lax.dynamic_update_slice(ask, source_row.reshape(1, targets), (0, 0))
    ask = lax.dynamic_update_slice(ask, source_block.reshape(1, targets), (1, 0))
    anywhere = pl.BlockSpec(memory_space=pl.ANY)
    vmem, bf16, f32 = pltpu.VMEM, jnp.bfloat16, jnp.float32
    dma = pltpu.SemaphoreType.DMA
    n_out = 3 * targets + 2
    mercator, one, two = pl.pallas_call(
        functools.partial(kernel, n_row, n_col),
        out_shape=(
            jax.ShapeDtypeStruct((TR_DEV * B, TC_DEV * B), f32),
            jax.ShapeDtypeStruct((TR_DEV * HALF, TC_DEV * HALF), f32),
            jax.ShapeDtypeStruct((B, B), f32),
        ),
        in_specs=[pl.BlockSpec(memory_space=pltpu.SMEM)] + [anywhere] * 4,
        out_specs=(anywhere,) * 3,
        scratch_shapes=[
            vmem((rows + 2 * PAD_R, cols + 2 * PAD_C), f32),
            vmem((2, rows, B), bf16),
            vmem((2, 8, 128), jnp.int32),
            pltpu.SMEM((2, 8, 128), jnp.int32),
            vmem((2, TC_DEV, TR_DEV, B, B), bf16),
            vmem((TR_DEV, TC_DEV, B, B), bf16),
            vmem((targets, B, B), bf16),
            vmem((targets, B, B), bf16),
            vmem((targets, 2, B, HALF), f32),
            vmem((targets // 2, 2, HALF, HALF), f32),
            vmem((HALF, B), f32),
            vmem((HALF, B), f32),
            vmem((HALF, B), f32),
        ]
        + [vmem((3, B, B), bf16)] * targets
        + [
            dma((3,)), dma((2,)), dma((2,)), dma, dma((8,)), dma((8,)),
            dma((2, TC_DEV, TR_DEV)), dma((2, TC_DEV, TR_DEV)), dma((2,)), dma((n_out,)),
        ],
        compiler_params=pltpu.CompilerParams(
            collective_id=0, has_side_effects=True, vmem_limit_bytes=44 * 1024 * 1024
        ),
        name="hillshade_tiles",
    )(ask, ask, elevation, row_weights, col_weights)
    return mercator, one, two.reshape(1, 1, B, B)


def solution(mesh):
    in_specs = (
        P("row", "col"),
        P(("row", "col"), None),
        P(("row", "col"), None),
        P(("row", "col"), None, None),
        P(("row", "col"), None, None),
    )
    out_specs = (P("row", "col"), P("row", "col"), P("row", "col", None, None))
    return jax.shard_map(
        functools.partial(per_device, mesh.shape["row"], mesh.shape["col"]),
        mesh=mesh, in_specs=in_specs, out_specs=out_specs, check_vma=False,
    )
```

time: 1240 us -> 108 us (0.09); the launches traced: 1220 us -> 108 us
  local copies, waits for them, and re-layouts: 1040 us -> 8.27 us
  other arithmetic: 149 us -> 0 us
  Pallas kernels: 0 us -> 98.8 us
  starting transfers between devices: 24.3 us -> 0 us
    gather x240 -> x0, local copies, waits for them, and re-layouts: 616 us -> none
    another operation x1 -> x0, local copies, waits for them, and re-layouts: 270 us -> none  [halve_image(): picture.reshape(pic_rows // 2, 2, pic_cols // 2, 2)]
    reduce_sum x2 -> x0, other arithmetic: 102 us -> none  [halve_image(): jnp.sum(picture.reshape(pic_rows // 2, 2, pic_cols // 2, 2), axis=(1, 3))]
    pallas_call x0 -> x1, Pallas kernels: none -> 98.8 us  [per_device(): pl.pallas_call(functools.partial(kernel, n_row, n_col), out_shape=(jax.Sh...]
    mul x1 -> x0, local copies, waits for them, and re-layouts: 68.6 us -> none  [halve_image(): jnp.sum(picture.reshape(pic_rows // 2, 2, pic_cols // 2, 2), axis=(1, 3))]
    concatenate x3 -> x0, local copies, waits for them, and re-layouts: 37.5 us -> none  [the longest x2 37.4 us: with_halo(): jnp.concatenate([lax.ppermute(tail, axis, [(i, (i + 1) % count) for i in...]
    unnamed x16 -> x7, local copies, waits for them, and re-layouts: 36.7 us -> 6.86 us
    ppermute x9 -> x0, starting transfers between devices: 24.3 us -> none  [the longest x4 16.6 us: with_halo(): lax.ppermute(tail, axis, [(i, (i + 1) % count) for i in range(ends)])]
  transfers between devices with their start and end apart: 9 -> 0, of which waited for: 1 -> 0; matrix products, arithmetic and copies ran while one was open for 36% -> 0% of each run, Pallas kernels for 0% -> 0%
where the time goes in v1:
time: 108 us
  Pallas kernels  98.8 us (91%)
  local copies, waits for them, and re-layouts  8.27 us (8%)
    pallas_call x1, Pallas kernels, per_device(): pl.pallas_call(functools.partial(kernel, n_row, n_col), out_shape=(jax.Sh...  98.8 us
    unnamed x7, local copies, waits for them, and re-layouts  6.86 us

profile of v1, /device:TPU:0, one launch (start us, length us, event | category | flops | bytes accessed | tf_op | source)
XLA Modules:
  0.0 107.7 jit_solution(10652725628405823214)
XLA Ops:
  0.6 0.7 dynamic_update_slice.6
  1.3 0.7 dynamic_update_slice.7.ask_ref.ask_hbm
  2.0 0.0 copy-start
  2.0 1.6 %copy-done = bf16[16,256,256]{2,1,0:T(8,128)(2,1)S(1)} copy-done((bf16[16,256,256]{2,1,0:T(8,128)(2,1)S(1)}, bf16[16,256,256]{2,1,0:T(8,128)(2,1)}, u32[]{:S(2)}) %copy-start) | copy-done | bytes 2097176
  3.6 0.0 copy-start.1
  3.6 1.6 %copy-done.1 = bf16[16,256,256]{2,1,0:T(8,128)(2,1)S(1)} copy-done((bf16[16,256,256]{2,1,0:T(8,128)(2,1)S(1)}, bf16[16,256,256]{2,1,0:T(8,128)(2,1)}, u32[]{:S(2)}) %copy-start.1) | copy-done | bytes 2097176
  5.2 98.8 %hillshade_tiles.1 = (f32[512,2048]{1,0:T(8,128)S(1)}, f32[256,1024]{1,0:T(8,128)S(1)}, f32[256,256]{1,0:T(8,128)S(1)}) custom-call(s32[8,128]{1,0:T(8,128)S(1)} %dynamic_update_slice.7.ask_ref.ask_hbm, s32[8,128]{1,0:T(8,128)S(1)} %dynamic_update_slice.7.ask_ref.ask_hbm, f32[1024,2048]{1,0:T(8,128)} %elev_hbm.1, bf16[16,256,256]{2,1,0:T(8,128)(2,1)S(1)} %copy-done, ...), custom_call_target="tpu_custom_call" | custom-call | tf_op jit(solution)/shard_map/hillshade_tiles/pallas_call | solution.py:302
  104.0 2.0 %copy.12 = f32[512,2048]{1,0:T(8,128)} copy(f32[512,2048]{1,0:T(8,128)S(1)} %get-tuple-element.12) | data formatting | bytes 8388608
  106.1 1.0 copy.13
  107.0 0.7 copy.14
Async XLA Ops:
  2.0 1.6 %copy-start = (bf16[16,256,256]{2,1,0:T(8,128)(2,1)S(1)}, bf16[16,256,256]{2,1,0:T(8,128)(2,1)}, u32[]{:S(2)}) copy-start(bf16[16,256,256]{2,1,0:T(8,128)(2,1)} %roww_hbm.1) | copy-start | bytes 6291460
  3.6 1.6 %copy-start.1 = (bf16[16,256,256]{2,1,0:T(8,128)(2,1)S(1)}, bf16[16,256,256]{2,1,0:T(8,128)(2,1)}, u32[]{:S(2)}) copy-start(bf16[16,256,256]{2,1,0:T(8,128)(2,1)} %colw_hbm.1) | copy-start | bytes 6291460

commit v2 on v1

--- a/solution.py
+++ b/solution.py
@@ -14,7 +14,7 @@
 TC_DEV = 8
 PAD_R = 8
 PAD_C = 128
-BAND = 32
+BAND = 64
 ORDER = (1, 2, 3, 4, 0, 5, 6, 7)
 READY = ((), (), (2,), (3,), (0, 1), (4,), (5,), (6, 7))
 
@@ -22,16 +22,18 @@
 MESH = pl.DeviceIdType.MESH
 
 
-def lit_of(east, south):
-    base = 0.25 * SUN_COS
-    straight = base / 8.0
-    slanted = 0.25 * 0.5 / 8.0
-    scale = lax.rsqrt(1.0 + (east * east + south * south) * (1.0 / 64.0))
-    lit = jnp.maximum(base + (east - south) * slanted, 0.0)
-    lit = lit + jnp.maximum(base + east * straight, 0.0)
-    lit = lit + jnp.maximum(base + (east + south) * slanted, 0.0)
-    lit = lit + jnp.maximum(base + south * straight, 0.0)
-    return lit * scale
+def shade(cells, band):
+    height, width = cells.shape
+    beside = cells + pltpu.roll(cells, width - 1, 1)
+    box = beside + pltpu.roll(beside, height - 1, 0)
+    box_up = pltpu.roll(box, 1, 0)
+    middle = slice(PAD_R, PAD_R + band), slice(PAD_C, width - PAD_C)
+    one = box[middle] - pltpu.roll(box_up, 1, 1)[middle]
+    two = box_up[middle] - pltpu.roll(box, 1, 1)[middle]
+    scale = lax.rsqrt((one * one + two * two) * 32.0 + 1024.0)
+    slanted = jnp.maximum(two, -8.0 * SUN_COS) + jnp.maximum(one, -8.0 * SUN_COS)
+    straight = jnp.maximum(one + two, -8.0) + jnp.maximum(one - two, -8.0)
+    return (straight * SUN_COS + (slanted + 32.0 * SUN_COS)) * scale
 
 
 def chosen(index, options):
@@ -51,9 +53,9 @@
 
 def kernel(
     n_row, n_col,
-    ask_ref, ask_hbm, elev_hbm, roww_hbm, colw_hbm,
+    srow_hbm, ask_hbm, elev_hbm, roww_hbm, colw_hbm,
     merc_hbm, one_hbm, two_hbm,
-    padded, shaded, asked, asked_s, sendbuf, merged, roww, colw, tiles, ones, two_own, two_send, two_got,
+    srow_ref, sblock_ref, padded, shaded, asked, asked_s, sendbuf, merged, roww, colw, tiles, ones, two_own, two_send, two_got,
     *rest,
 ):
     recv = rest[:16]
@@ -75,9 +77,24 @@
     def got_col(m):
         return (last - m) + parity * (2 * m - last)
 
-    inner = padded.at[pl.ds(PAD_R, rows), pl.ds(PAD_C, cols)]
-    load_elev = pltpu.make_async_copy(elev_hbm, inner, load_sem.at[0])
-    load_elev.start()
+    def load_block(m):
+        lane = pl.multiple_of(sent_col(m) * B, B)
+        return pltpu.make_async_copy(
+            elev_hbm.at[:, pl.ds(lane, B)],
+            padded.at[pl.ds(PAD_R, rows), pl.ds(lane + PAD_C, B)],
+            load_sem.at[m],
+        )
+
+    loads = {m: load_block(m) for m in (1, 0, 2, 3, 4, 5, 6, 7)}
+    for copy in loads.values():
+        copy.start()
+
+    numbers = [
+        pltpu.make_async_copy(srow_hbm, srow_ref, ask_local.at[1]),
+        pltpu.make_async_copy(ask_hbm, sblock_ref, ask_local.at[2]),
+    ]
+    for copy in numbers:
+        copy.start()
 
     around = [(up, col), (down, col), (row, left), (row, right), (up, left), (up, right), (down, left), (down, right)]
     barrier = pltpu.get_barrier_semaphore()
@@ -119,32 +136,35 @@
     ]
     for copy in halos:
         copy.start()
-    load_roww = pltpu.make_async_copy(roww_hbm, roww, load_sem.at[1])
-    load_colw = pltpu.make_async_copy(colw_hbm, colw, load_sem.at[2])
+    load_roww = pltpu.make_async_copy(roww_hbm, roww, load_sem.at[TC_DEV])
+    load_colw = pltpu.make_async_copy(colw_hbm, colw, load_sem.at[TC_DEV + 1])
     load_roww.start()
     load_colw.start()
-
-    for copy in asks:
-        copy.wait_recv()
-    to_scalar = pltpu.make_async_copy(asked, asked_s, ask_local)
-    to_scalar.start()
-    load_elev.wait()
-    halos[0].wait_recv()
-    halos[1].wait_recv()
 
     def clear(where):
         shape = tuple(s.size for s in where)
         padded[where] = jnp.zeros(shape, jnp.float32)
 
-    @pl.when(row == 0)
-    def _():
-        clear((top, mid_c))
-
-    @pl.when(row == n_row - 1)
-    def _():
-        clear((bottom, mid_c))
-
-    to_scalar.wait()
+    def first_halo():
+        for copy in asks:
+            copy.wait_recv()
+        to_scalar.start()
+        halos[0].wait_recv()
+        halos[1].wait_recv()
+
+        @pl.when(row == 0)
+        def _():
+            clear((top, mid_c))
+
+        @pl.when(row == n_row - 1)
+        def _():
+            clear((bottom, mid_c))
+
+        for copy in [to_scalar] + numbers:
+            copy.wait()
+
+    to_scalar = pltpu.make_async_copy(asked, asked_s, ask_local.at[0])
+    arrived = set()
 
     pool_rows = lax.broadcasted_iota(jnp.int32, (B, HALF), 0)
     pool_cols = lax.broadcasted_iota(jnp.int32, (B, HALF), 1)
@@ -186,22 +206,24 @@
         def shade_band(i, carry, lane=lane, slot=slot):
             start = pl.multiple_of(i * BAND, BAND)
             cells = padded[pl.ds(start, BAND + 2 * PAD_R), pl.ds(lane, B + 2 * PAD_C)]
-            before = cells[:, PAD_C - 1 : PAD_C - 1 + B]
-            here = cells[:, PAD_C : PAD_C + B]
-            after = cells[:, PAD_C + 1 : PAD_C + 1 + B]
-            across = after - before
-            along = (before + after) + (here + here)
-            middle = across[PAD_R : PAD_R + BAND]
-            east8 = (across[PAD_R - 1 : PAD_R - 1 + BAND] + across[PAD_R + 1 : PAD_R + 1 + BAND]) + (middle + middle)
-            south8 = along[PAD_R + 1 : PAD_R + 1 + BAND] - along[PAD_R - 1 : PAD_R - 1 + BAND]
-            shaded[slot, pl.ds(start, BAND), :] = lit_of(east8, south8).astype(jnp.bfloat16)
+            shaded[slot, pl.ds(start, BAND), :] = shade(cells, BAND).astype(jnp.bfloat16)
             return carry
 
-        lax.fori_loop(0, rows // BAND, shade_band, 0)
+        for k in (m - 1, m, m + 1):
+            if 0 <= k <= last and k not in arrived:
+                loads[k].wait()
+                arrived.add(k)
+        bands = rows // BAND
+        if step == 0:
+            lax.fori_loop(1, bands - 1, shade_band, 0, unroll=2)
+            first_halo()
+            lax.fori_loop(0, 2, lambda i, c: shade_band(i * (bands - 1), c), 0)
+        else:
+            lax.fori_loop(0, bands, shade_band, 0, unroll=2)
         for g in range(TR_DEV):
             for side in range(2):
                 sendbuf[side, m, g] = chosen(
-                    lax.div(asked_s[side, 1, g * TC_DEV], TC_DEV),
+                    lax.div(asked_s[side, 0, g * TC_DEV], TC_DEV),
                     [shaded[slot, k * B : (k + 1) * B, :] for k in range(rows // B)],
                 )
         for g in range(TR_DEV):
@@ -217,7 +239,7 @@
                 strips.append(((step, g, side), copy))
         for g in range(TR_DEV):
             recv[(last - m) * TR_DEV + g][1] = chosen(
-                lax.div(ask_ref[1, g * TC_DEV], TC_DEV),
+                lax.div(sblock_ref[0, g * TC_DEV], TC_DEV),
                 [shaded[slot, k * B : (k + 1) * B, :] for k in range(rows // B)],
             )
     strips = dict(strips)
@@ -237,7 +259,7 @@
         t = g * TC_DEV + j
         place = g * TC_DEV + m
         near = [k for k in (m - 1, m, m + 1) if 0 <= k <= last]
-        wanted = lax.rem(ask_ref[1, t], TC_DEV)
+        wanted = lax.rem(sblock_ref[0, t], TC_DEV)
         where = wanted + (1 - parity) * (last - 2 * wanted)
         source = chosen(where - near[0], [merged[g, k] for k in near])
         half_done = jnp.dot(roww[t], source, preferred_element_type=jnp.float32).astype(jnp.bfloat16)
@@ -269,7 +291,7 @@
         for g in range(TR_DEV):
             strips[step, g, 0].wait_recv()
             strips[step, g, 1].wait_recv()
-            side = ask_ref[0, g * TC_DEV] - row + 1
+            side = srow_ref[0, g * TC_DEV] - row + 1
             merged[g, m] = chosen(side, [recv[m * TR_DEV + g][k] for k in range(3)])
             for target in READY[step]:
                 make_target(g, target)
@@ -292,10 +314,11 @@
 def per_device(n_row, n_col, elevation, source_row, source_block, row_weights, col_weights):
     rows, cols = elevation.shape
     targets = source_row.shape[0]
-    ask = jnp.zeros((8, 128), jnp.int32)
-    ask = lax.dynamic_update_slice(ask, source_row.reshape(1, targets), (0, 0))
-    ask = lax.dynamic_update_slice(ask, source_block.reshape(1, targets), (1, 0))
+    source_row = source_row.reshape(1, targets)
+    source_block = source_block.reshape(1, targets)
     anywhere = pl.BlockSpec(memory_space=pl.ANY)
+    in_hbm = pl.BlockSpec(memory_space=pltpu.HBM)
+    operands = (source_row, source_block, elevation, row_weights, col_weights)
     vmem, bf16, f32 = pltpu.VMEM, jnp.bfloat16, jnp.float32
     dma = pltpu.SemaphoreType.DMA
     n_out = 3 * targets + 2
@@ -306,13 +329,15 @@
             jax.ShapeDtypeStruct((TR_DEV * HALF, TC_DEV * HALF), f32),
             jax.ShapeDtypeStruct((B, B), f32),
         ),
-        in_specs=[pl.BlockSpec(memory_space=pltpu.SMEM)] + [anywhere] * 4,
+        in_specs=[in_hbm] * len(operands),
         out_specs=(anywhere,) * 3,
         scratch_shapes=[
+            pltpu.SMEM((1, targets), jnp.int32),
+            pltpu.SMEM((1, targets), jnp.int32),
             vmem((rows + 2 * PAD_R, cols + 2 * PAD_C), f32),
             vmem((2, rows, B), bf16),
-            vmem((2, 8, 128), jnp.int32),
-            pltpu.SMEM((2, 8, 128), jnp.int32),
+            vmem((2, 1, targets), jnp.int32),
+            pltpu.SMEM((2, 1, targets), jnp.int32),
             vmem((2, TC_DEV, TR_DEV, B, B), bf16),
             vmem((TR_DEV, TC_DEV, B, B), bf16),
             vmem((targets, B, B), bf16),
@@ -325,14 +350,14 @@
         ]
         + [vmem((3, B, B), bf16)] * targets
         + [
-            dma((3,)), dma((2,)), dma((2,)), dma, dma((8,)), dma((8,)),
+            dma((TC_DEV + 2,)), dma((2,)), dma((2,)), dma((3,)), dma((8,)), dma((8,)),
             dma((2, TC_DEV, TR_DEV)), dma((2, TC_DEV, TR_DEV)), dma((2,)), dma((n_out,)),
         ],
         compiler_params=pltpu.CompilerParams(
             collective_id=0, has_side_effects=True, vmem_limit_bytes=44 * 1024 * 1024
         ),
         name="hillshade_tiles",
-    )(ask, ask, elevation, row_weights, col_weights)
+    )(*(pltpu.with_memory_space_constraint(x, pltpu.HBM) for x in operands))
     return mercator, one, two.reshape(1, 1, B, B)
 
 

time: 108 us -> 68 us (0.63)
  Pallas kernels: 98.8 us -> 63.6 us
  local copies, waits for them, and re-layouts: 8.27 us -> 3.69 us
    pallas_call x1, Pallas kernels: 98.8 us -> 63.6 us  [per_device(): pl.pallas_call(functools.partial(kernel, n_row, n_col), out_shape=(jax.Sh...]
    unnamed x7 -> x3, local copies, waits for them, and re-layouts: 6.86 us -> 3.69 us
    dynamic_update_slice x2 -> x0, local copies, waits for them, and re-layouts: 1.41 us -> none  [the longest x1 0.74 us: per_device(): lax.dynamic_update_slice(ask, source_block.reshape(1, targets), (1, 0))]
where the time goes in v2:
time: 68 us; the launch traced here: 67.9 us
  Pallas kernels  63.6 us (94%)
  local copies, waits for them, and re-layouts  3.69 us (5%)
    pallas_call x1, Pallas kernels, per_device(): pl.pallas_call(functools.partial(kernel, n_row, n_col), out_shape=(jax.Sh...  63.6 us
    unnamed x3, local copies, waits for them, and re-layouts  3.69 us

profile of v2, /device:TPU:0, one launch (start us, length us, event | category | flops | bytes accessed | tf_op | source)
XLA Modules:
  0.0 67.9 jit_solution(12659239046555135654)
XLA Ops:
  0.6 63.6 %hillshade_tiles.1 = (f32[512,2048]{1,0:T(8,128)S(1)}, f32[256,1024]{1,0:T(8,128)S(1)}, f32[256,256]{1,0:T(8,128)S(1)}) custom-call(s32[1,16]{1,0:T(1,128)} %bitcast.4, s32[1,16]{1,0:T(1,128)} %bitcast.5, f32[1024,2048]{1,0:T(8,128)} %elev_hbm.1, bf16[16,256,256]{2,1,0:T(8,128)(2,1)} %roww_hbm.1, bf16[16,256,256]{2,1,0:T(8,128)(2,1)} %colw_hbm.1), custom_call_target="tpu_custom_call" | custom-call | tf_op jit(solution)/shard_map/hillshade_tiles/pallas_call | solution.py:325
  64.2 2.0 %copy.11 = f32[512,2048]{1,0:T(8,128)} copy(f32[512,2048]{1,0:T(8,128)S(1)} %get-tuple-element.12) | data formatting | bytes 8388608
  66.2 1.0 %copy.12 = f32[256,1024]{1,0:T(8,128)} copy(f32[256,1024]{1,0:T(8,128)S(1)} %get-tuple-element.13) | data formatting | bytes 2097152
  67.2 0.7 %copy.13 = f32[1,1,256,256]{3,2,1,0:T(8,128)} copy(f32[1,1,256,256]{3,2,1,0:T(8,128)S(1)} %bitcast.3) | data formatting | bytes 524288

commit v3 on v2

--- a/solution.py
+++ b/solution.py
@@ -10,6 +10,7 @@
 
 B = 256
 HALF = B // 2
+QUARTER = B // 4
 TR_DEV = 2
 TC_DEV = 8
 PAD_R = 8
@@ -17,6 +18,7 @@
 BAND = 64
 ORDER = (1, 2, 3, 4, 0, 5, 6, 7)
 READY = ((), (), (2,), (3,), (0, 1), (4,), (5,), (6, 7))
+LATE = ((1, 6), (1, 7))
 
 SUN_COS = math.cos(math.pi / 4.0)
 MESH = pl.DeviceIdType.MESH
@@ -51,11 +53,30 @@
     )
 
 
+def got_col(m, parity):
+    return (TC_DEV - 1 - m) + parity * (2 * m - (TC_DEV - 1))
+
+
+def render(row_weights, source, col_weights):
+    inner_rows = jnp.dot(row_weights, source, preferred_element_type=jnp.float32).astype(jnp.bfloat16)
+    return jnp.dot(inner_rows, col_weights, preferred_element_type=jnp.float32)
+
+
+def row_pairs(ref, where, count):
+    return ref[(*where, pl.ds(0, count, stride=2), slice(None))] + ref[(*where, pl.ds(1, count, stride=2), slice(None))]
+
+
+def pooling_matrix():
+    rows = lax.broadcasted_iota(jnp.int32, (B, HALF), 0)
+    cols = lax.broadcasted_iota(jnp.int32, (B, HALF), 1)
+    return jnp.where(rows // 2 == cols, 0.25, 0.0).astype(jnp.bfloat16)
+
+
 def kernel(
     n_row, n_col,
     srow_hbm, ask_hbm, elev_hbm, roww_hbm, colw_hbm,
-    merc_hbm, one_hbm, two_hbm,
-    srow_ref, sblock_ref, padded, shaded, asked, asked_s, sendbuf, merged, roww, colw, tiles, ones, two_own, two_send, two_got,
+    merc_out, one_out, two_out, two_got, late_out,
+    srow_ref, sblock_ref, padded, shaded, asked_s, sendbuf, merged, roww, colw, tiles, ones, two_own, two_send, late_source,
     *rest,
 ):
     recv = rest[:16]
@@ -74,9 +95,6 @@
     def sent_col(m):
         return m + parity * (last - 2 * m)
 
-    def got_col(m):
-        return (last - m) + parity * (2 * m - last)
-
     def load_block(m):
         lane = pl.multiple_of(sent_col(m) * B, B)
         return pltpu.make_async_copy(
@@ -96,7 +114,7 @@
     for copy in numbers:
         copy.start()
 
-    around = [(up, col), (down, col), (row, left), (row, right), (up, left), (up, right), (down, left), (down, right)]
+    around = [(up, col), (down, col), (row, left), (row, right)]
     barrier = pltpu.get_barrier_semaphore()
     for device in around:
         pl.semaphore_signal(barrier, inc=1, device_id=device, device_id_type=MESH)
@@ -108,34 +126,29 @@
         )
 
     asks = [
-        remote(ask_hbm, asked.at[1], ask_send.at[0], ask_recv.at[1], (up, col)),
-        remote(ask_hbm, asked.at[0], ask_send.at[1], ask_recv.at[0], (down, col)),
+        remote(ask_hbm, asked_s.at[1], ask_send.at[0], ask_recv.at[1], (up, col)),
+        remote(ask_hbm, asked_s.at[0], ask_send.at[1], ask_recv.at[0], (down, col)),
     ]
     for copy in asks:
         copy.start()
 
     top, bottom = pl.ds(0, PAD_R), pl.ds(PAD_R + rows, PAD_R)
-    mid_r, mid_c = pl.ds(PAD_R, rows), pl.ds(PAD_C, cols)
+    mid_c = pl.ds(PAD_C, cols)
     west, east = pl.ds(0, PAD_C), pl.ds(PAD_C + cols, PAD_C)
     first_r, last_r = pl.ds(0, PAD_R), pl.ds(rows - PAD_R, PAD_R)
-    first_c, last_c = pl.ds(0, PAD_C), pl.ds(cols - PAD_C, PAD_C)
-    all_r, all_c = pl.ds(0, rows), pl.ds(0, cols)
-    halo_plan = [
-        ((first_r, all_c), (bottom, mid_c), (up, col)),
-        ((last_r, all_c), (top, mid_c), (down, col)),
-        ((all_r, first_c), (mid_r, east), (row, left)),
-        ((all_r, last_c), (mid_r, west), (row, right)),
-        ((first_r, first_c), (bottom, east), (up, left)),
-        ((first_r, last_c), (bottom, west), (up, right)),
-        ((last_r, first_c), (top, east), (down, left)),
-        ((last_r, last_c), (top, west), (down, right)),
-    ]
+    all_c = pl.ds(0, cols)
     halos = [
-        remote(elev_hbm.at[src], padded.at[dst], halo_send.at[i], halo_recv.at[i], device)
-        for i, (src, dst, device) in enumerate(halo_plan)
+        remote(elev_hbm.at[first_r, all_c], padded.at[bottom, mid_c], halo_send.at[0], halo_recv.at[0], (up, col)),
+        remote(elev_hbm.at[last_r, all_c], padded.at[top, mid_c], halo_send.at[1], halo_recv.at[1], (down, col)),
     ]
     for copy in halos:
         copy.start()
+    every_r = pl.ds(0, rows + 2 * PAD_R)
+    inner_west, inner_east = pl.ds(PAD_C, PAD_C), pl.ds(cols, PAD_C)
+    sides = [
+        remote(padded.at[every_r, inner_west], padded.at[every_r, east], halo_send.at[2], halo_recv.at[2], (row, left)),
+        remote(padded.at[every_r, inner_east], padded.at[every_r, west], halo_send.at[3], halo_recv.at[3], (row, right)),
+    ]
     load_roww = pltpu.make_async_copy(roww_hbm, roww, load_sem.at[TC_DEV])
     load_colw = pltpu.make_async_copy(colw_hbm, colw, load_sem.at[TC_DEV + 1])
     load_roww.start()
@@ -148,7 +161,6 @@
     def first_halo():
         for copy in asks:
             copy.wait_recv()
-        to_scalar.start()
         halos[0].wait_recv()
         halos[1].wait_recv()
 
@@ -160,45 +172,32 @@
         def _():
             clear((bottom, mid_c))
 
-        for copy in [to_scalar] + numbers:
+        for copy in numbers:
             copy.wait()
 
-    to_scalar = pltpu.make_async_copy(asked, asked_s, ask_local.at[0])
     arrived = set()
 
-    pool_rows = lax.broadcasted_iota(jnp.int32, (B, HALF), 0)
-    pool_cols = lax.broadcasted_iota(jnp.int32, (B, HALF), 1)
-    pool = jnp.where(pool_rows // 2 == pool_cols, 0.25, 0.0).astype(jnp.bfloat16)
-
+    pool = pooling_matrix()
     strips = []
     for step, m in enumerate(ORDER):
+        if step == 2:
+            for k in (0, last):
+                if k not in arrived:
+                    loads[k].wait()
+                    arrived.add(k)
+            for copy in sides:
+                copy.start()
         if step == 4:
-            for copy in halos[2:]:
+            for copy in sides:
                 copy.wait_recv()
 
             @pl.when(col == 0)
             def _():
-                clear((mid_r, west))
+                clear((every_r, west))
 
             @pl.when(col == n_col - 1)
             def _():
-                clear((mid_r, east))
-
-            @pl.when((row == 0) | (col == 0))
-            def _():
-                clear((top, west))
-
-            @pl.when((row == 0) | (col == n_col - 1))
-            def _():
-                clear((top, east))
-
-            @pl.when((row == n_row - 1) | (col == 0))
-            def _():
-                clear((bottom, west))
-
-            @pl.when((row == n_row - 1) | (col == n_col - 1))
-            def _():
-                clear((bottom, east))
+                clear((every_r, east))
 
         lane = pl.multiple_of(sent_col(m) * B, PAD_C)
         slot = step % 2
@@ -255,36 +254,45 @@
         outs.append(copy)
 
     def make_target(g, m):
-        j = got_col(m)
+        j = got_col(m, parity)
         t = g * TC_DEV + j
         place = g * TC_DEV + m
         near = [k for k in (m - 1, m, m + 1) if 0 <= k <= last]
         wanted = lax.rem(sblock_ref[0, t], TC_DEV)
         where = wanted + (1 - parity) * (last - 2 * wanted)
         source = chosen(where - near[0], [merged[g, k] for k in near])
-        half_done = jnp.dot(roww[t], source, preferred_element_type=jnp.float32).astype(jnp.bfloat16)
-        tile = jnp.dot(half_done, colw[t], preferred_element_type=jnp.float32)
+        if (g, m) in LATE:
+            spot = LATE.index((g, m))
+            late_source[spot] = source
+            out_copy(late_source.at[spot], late_out.at[0, spot])
+            return
+        tile = render(roww[t], source, colw[t])
         sums = []
         for half in range(2):
             tiles[place, half] = tile[:, half * HALF : (half + 1) * HALF]
             lane = pl.multiple_of(j * B + half * HALF, HALF)
-            out_copy(tiles.at[place, half], merc_hbm.at[pl.ds(g * B, B), pl.ds(lane, HALF)])
-            sums.append(tiles[place, half, pl.ds(0, HALF, stride=2), :] + tiles[place, half, pl.ds(1, HALF, stride=2), :])
+            out_copy(tiles.at[place, half], merc_out.at[pl.ds(g * B, B), pl.ds(lane, HALF)])
+            sums.append(row_pairs(tiles, (place, half), HALF))
         where = (g * 4 + m // 2, lax.rem(j, 2))
         ones[where] = pooled(jnp.concatenate(sums, axis=1), pool)
         lane = pl.multiple_of(j * HALF, HALF)
-        out_copy(ones.at[where], one_hbm.at[pl.ds(g * HALF, HALF), pl.ds(lane, HALF)])
+        out_copy(ones.at[where], one_out.at[pl.ds(g * HALF, HALF), pl.ds(lane, HALF)])
 
     def make_coarse(g, pair):
-        actual = lax.div(got_col(2 * pair), 2)
-        quarter = HALF // 2
-        sums = [
-            ones[g * 4 + pair, half, pl.ds(0, quarter, stride=2), :] + ones[g * 4 + pair, half, pl.ds(1, quarter, stride=2), :]
-            for half in range(2)
-        ]
+        actual = lax.div(got_col(2 * pair, parity), 2)
         lane = pl.multiple_of(lax.rem(actual, 2) * HALF, HALF)
-        dest = two_send if pair < 2 else two_own
-        dest[pl.ds(g * quarter, quarter), pl.ds(lane, HALF)] = pooled(jnp.concatenate(sums, axis=1), pool)
+        sums = [row_pairs(ones, (g * 4 + pair, half), QUARTER) for half in range(2)]
+        block = pooled(jnp.concatenate(sums, axis=1), pool)
+        where = pl.ds(g * QUARTER, QUARTER), pl.ds(lane, HALF)
+        if pair < 2:
+            two_send[where] = block.astype(jnp.bfloat16)
+        else:
+            two_own[where] = block
+
+    for spot, (g, m) in enumerate(LATE):
+        t = g * TC_DEV + got_col(m, parity)
+        out_copy(roww.at[t], late_out.at[1, spot])
+        out_copy(colw.at[t], late_out.at[2, spot])
 
     done = set()
     for step, m in enumerate(ORDER):
@@ -297,18 +305,63 @@
                 make_target(g, target)
                 done.add((g, target))
                 pair = target // 2
-                if (g, 2 * pair) in done and (g, 2 * pair + 1) in done:
+                both = (g, 2 * pair), (g, 2 * pair + 1)
+                if all(x in done and x not in LATE for x in both):
                     make_coarse(g, pair)
         if step == 4:
             two_copy.start()
-    out_copy(two_own, two_hbm.at[pl.ds(pl.multiple_of(parity * (HALF), HALF), HALF), :])
+    out_copy(two_own, two_out)
     two_copy.wait_recv()
-    out_copy(two_got, two_hbm.at[pl.ds(pl.multiple_of((1 - parity) * (HALF), HALF), HALF), :])
     for copy in outs:
         copy.wait()
     two_copy.wait_send()
-    for copy in asks + halos + list(strips.values()):
+    for copy in asks + halos + sides + list(strips.values()):
         copy.wait_send()
+
+
+def finish(merc_in, one_in, two_in, two_got, late, merc_hbm, one_hbm, two_hbm, tiles, ones, coarse, other, sem):
+    parity = lax.rem(lax.axis_index("row"), 2)
+    copies = []
+
+    def start(src, dst):
+        copy = pltpu.make_async_copy(src, dst, sem.at[len(copies)])
+        copy.start()
+        copies.append(copy)
+
+    def same(src, dst, rows, cols):
+        start(src.at[rows, cols], dst.at[rows, cols])
+
+    width = TC_DEV * B
+    most = 6 * B
+    same(merc_in, merc_hbm, pl.ds(0, B), pl.ds(0, width))
+    same(merc_in, merc_hbm, pl.ds(B, B), pl.ds(pl.multiple_of((1 - parity) * (width - most), B), most))
+    same(one_in, one_hbm, pl.ds(0, HALF), pl.ds(0, width // 2))
+    same(one_in, one_hbm, pl.ds(HALF, HALF), pl.ds(pl.multiple_of((1 - parity) * (width - most) // 2, HALF), most // 2))
+    own = parity * HALF
+    start(two_in.at[pl.ds(0, QUARTER), :], two_hbm.at[pl.ds(pl.multiple_of(own, QUARTER), QUARTER), :])
+    low = pl.ds(pl.multiple_of(own + QUARTER, QUARTER), QUARTER)
+    lane = pl.ds(pl.multiple_of((1 - parity) * HALF, HALF), HALF)
+    start(two_in.at[pl.ds(QUARTER, QUARTER), lane], two_hbm.at[low, lane])
+    other[...] = two_got[...].astype(jnp.float32)
+    start(other, two_hbm.at[pl.ds(pl.multiple_of((1 - parity) * HALF, HALF), HALF), :])
+
+    pool = pooling_matrix()
+    for spot, (g, m) in enumerate(LATE):
+        j = got_col(m, parity)
+        tile = render(late[1, spot], late[0, spot], late[2, spot])
+        sums = []
+        for half in range(2):
+            tiles[spot, half] = tile[:, half * HALF : (half + 1) * HALF]
+            lane = pl.multiple_of(j * B + half * HALF, HALF)
+            start(tiles.at[spot, half], merc_hbm.at[pl.ds(g * B, B), pl.ds(lane, HALF)])
+            sums.append(row_pairs(tiles, (spot, half), HALF))
+        ones[lax.rem(j, 2)] = pooled(jnp.concatenate(sums, axis=1), pool)
+        start(ones.at[lax.rem(j, 2)], one_hbm.at[pl.ds(g * HALF, HALF), pl.ds(pl.multiple_of(j * HALF, HALF), HALF)])
+    sums = [row_pairs(ones, (half,), QUARTER) for half in range(2)]
+    coarse[...] = pooled(jnp.concatenate(sums, axis=1), pool)
+    start(coarse, two_hbm.at[low, pl.ds(pl.multiple_of(parity * HALF, HALF), HALF)])
+    for copy in copies:
+        copy.wait()
 
 
 def per_device(n_row, n_col, elevation, source_row, source_block, row_weights, col_weights):
@@ -321,22 +374,27 @@
     operands = (source_row, source_block, elevation, row_weights, col_weights)
     vmem, bf16, f32 = pltpu.VMEM, jnp.bfloat16, jnp.float32
     dma = pltpu.SemaphoreType.DMA
-    n_out = 3 * targets + 2
-    mercator, one, two = pl.pallas_call(
+    n_out = 3 * targets + 1
+    images = (
+        jax.ShapeDtypeStruct((TR_DEV * B, TC_DEV * B), f32),
+        jax.ShapeDtypeStruct((TR_DEV * HALF, TC_DEV * HALF), f32),
+        jax.ShapeDtypeStruct((B, B), f32),
+    )
+    parts = pl.pallas_call(
         functools.partial(kernel, n_row, n_col),
         out_shape=(
-            jax.ShapeDtypeStruct((TR_DEV * B, TC_DEV * B), f32),
-            jax.ShapeDtypeStruct((TR_DEV * HALF, TC_DEV * HALF), f32),
-            jax.ShapeDtypeStruct((B, B), f32),
+            *images[:2],
+            jax.ShapeDtypeStruct((HALF, B), f32),
+            jax.ShapeDtypeStruct((HALF, B), bf16),
+            jax.ShapeDtypeStruct((3, len(LATE), B, B), bf16),
         ),
         in_specs=[in_hbm] * len(operands),
-        out_specs=(anywhere,) * 3,
+        out_specs=(anywhere,) * 5,
         scratch_shapes=[
             pltpu.SMEM((1, targets), jnp.int32),
             pltpu.SMEM((1, targets), jnp.int32),
             vmem((rows + 2 * PAD_R, cols + 2 * PAD_C), f32),
             vmem((2, rows, B), bf16),
-            vmem((2, 1, targets), jnp.int32),
             pltpu.SMEM((2, 1, targets), jnp.int32),
             vmem((2, TC_DEV, TR_DEV, B, B), bf16),
             vmem((TR_DEV, TC_DEV, B, B), bf16),
@@ -345,12 +403,12 @@
             vmem((targets, 2, B, HALF), f32),
             vmem((targets // 2, 2, HALF, HALF), f32),
             vmem((HALF, B), f32),
-            vmem((HALF, B), f32),
-            vmem((HALF, B), f32),
+            vmem((HALF, B), bf16),
+            vmem((len(LATE), B, B), bf16),
         ]
         + [vmem((3, B, B), bf16)] * targets
         + [
-            dma((TC_DEV + 2,)), dma((2,)), dma((2,)), dma((3,)), dma((8,)), dma((8,)),
+            dma((TC_DEV + 2,)), dma((2,)), dma((2,)), dma((3,)), dma((4,)), dma((4,)),
             dma((2, TC_DEV, TR_DEV)), dma((2, TC_DEV, TR_DEV)), dma((2,)), dma((n_out,)),
         ],
         compiler_params=pltpu.CompilerParams(
@@ -358,6 +416,21 @@
         ),
         name="hillshade_tiles",
     )(*(pltpu.with_memory_space_constraint(x, pltpu.HBM) for x in operands))
+    mercator, one, two = pl.pallas_call(
+        finish,
+        out_shape=images,
+        in_specs=[anywhere] * 3 + [pl.BlockSpec(memory_space=vmem)] * 2,
+        out_specs=(in_hbm,) * 3,
+        scratch_shapes=[
+            vmem((len(LATE), 2, B, HALF), f32),
+            vmem((2, HALF, HALF), f32),
+            vmem((QUARTER, HALF), f32),
+            vmem((HALF, B), f32),
+            dma((7 + 3 * len(LATE) + 1,)),
+        ],
+        compiler_params=pltpu.CompilerParams(vmem_limit_bytes=8 * 1024 * 1024),
+        name="hillshade_finish",
+    )(*parts)
     return mercator, one, two.reshape(1, 1, B, B)
 
 

time: 68 us -> 63.7 us (0.937)
  local copies, waits for them, and re-layouts: 3.69 us -> 0 us
  Pallas kernels: 63.6 us -> 62.9 us
    unnamed x3 -> x0, local copies, waits for them, and re-layouts: 3.69 us -> none
    pallas_call x1 -> x2, Pallas kernels: 63.6 us -> 62.9 us  [the longest x1 60.4 us: per_device(): pl.pallas_call(functools.partial(kernel, n_row, n_col), out_shape=(*image...]
where the time goes in v3:
time: 63.7 us; the launch traced here: 63.6 us
  Pallas kernels  62.9 us (99%)
  between operations  0.64 us (1%)
    pallas_call x1, Pallas kernels, per_device(): pl.pallas_call(functools.partial(kernel, n_row, n_col), out_shape=(*image...  60.4 us
    pallas_call x1, Pallas kernels, per_device(): pl.pallas_call(finish, out_shape=images, in_specs=[anywhere] * 3 + [pl.Bl...  2.53 us

profile of v3, /device:TPU:0, one launch (start us, length us, event | category | flops | bytes accessed | tf_op | source)
XLA Modules:
  0.0 63.6 jit_solution(14968664744205003723)
XLA Ops:
  0.6 60.4 %hillshade_tiles.1 = (f32[512,2048]{1,0:T(8,128)S(1)}, f32[256,1024]{1,0:T(8,128)S(1)}, f32[128,256]{1,0:T(8,128)S(1)}, bf16[128,256]{1,0:T(8,128)(2,1)S(1)}, bf16[3,2,256,256]{3,2,1,0:T(8,128)(2,1)S(1)}) custom-call(s32[1,16]{1,0:T(1,128)} %bitcast.3, s32[1,16]{1,0:T(1,128)} %bitcast.4, f32[1024,2048]{1,0:T(8,128)} %elev_hbm.1, ...), custom_call_target="tpu_custom_call" | custom-call | tf_op jit(solution)/shard_map/hillshade_tiles/pallas_call | solution.py:383
  61.0 2.5 %hillshade_finish.1 = (f32[512,2048]{1,0:T(8,128)}, f32[256,1024]{1,0:T(8,128)}, f32[256,256]{1,0:T(8,128)}) custom-call(f32[512,2048]{1,0:T(8,128)S(1)} %get-tuple-element.11.merc_in, f32[256,1024]{1,0:T(8,128)S(1)} %get-tuple-element.12.one_in, f32[128,256]{1,0:T(8,128)S(1)} %get-tuple-element.13.two_in, bf16[128,256]{1,0:T(8,128)(2,1)S(1)} %get-tuple-element.14.two_got, ...), custom_call_target="tpu_custom_call" | custom-call | tf_op jit(solution)/shard_map/hillshade_finish/pallas_call | solution.py:419

commit v4 on v3

--- a/solution.py
+++ b/solution.py
@@ -76,11 +76,11 @@
     n_row, n_col,
     srow_hbm, ask_hbm, elev_hbm, roww_hbm, colw_hbm,
     merc_out, one_out, two_out, two_got, late_out,
-    srow_ref, sblock_ref, padded, shaded, asked_s, sendbuf, merged, roww, colw, tiles, ones, two_own, two_send, late_source,
+    srow_ref, sblock_ref, padded, shaded, asked_s, sendbuf, merged, roww, colw, tiles, ones, two_own, two_send, late_source, blind_send, blind_got,
     *rest,
 ):
     recv = rest[:16]
-    (load_sem, ask_send, ask_recv, ask_local, halo_send, halo_recv,
+    (first_sem, load_sem, early_send, early_recv, blind_sems, ask_send, ask_recv, ask_local, halo_send, halo_recv,
      strip_send, strip_recv, two_sems, out_sem) = rest[16:]
     row = lax.axis_index("row")
     col = lax.axis_index("col")
@@ -95,21 +95,33 @@
     def sent_col(m):
         return m + parity * (last - 2 * m)
 
-    def load_block(m):
-        lane = pl.multiple_of(sent_col(m) * B, B)
+    pieces = rows // B
+    span = B + 2 * PAD_C
+    first_lane = pl.multiple_of(sent_col(ORDER[0]) * B - PAD_C, PAD_C)
+    narrow, wide = PAD_C, cols - span - PAD_C
+
+    def load(row_start, height, lane, width, sem):
         return pltpu.make_async_copy(
-            elev_hbm.at[:, pl.ds(lane, B)],
-            padded.at[pl.ds(PAD_R, rows), pl.ds(lane + PAD_C, B)],
-            load_sem.at[m],
+            elev_hbm.at[pl.ds(row_start, height), pl.ds(lane, width)],
+            padded.at[pl.ds(row_start + PAD_R, height), pl.ds(lane + PAD_C, width)],
+            sem,
         )
 
-    loads = {m: load_block(m) for m in (1, 0, 2, 3, 4, 5, 6, 7)}
-    for copy in loads.values():
-        copy.start()
+    def first_load(i):
+        return load(pl.multiple_of(i * B, B), B, first_lane, span, first_sem.at[i])
+
+    for i in range(pieces):
+        first_load(i).start()
+    rest = [
+        load(0, rows, pl.multiple_of((1 - parity) * (narrow + span), PAD_C), wide, load_sem.at[0]),
+        load(0, rows, pl.multiple_of(parity * (cols - narrow), PAD_C), narrow, load_sem.at[1]),
+        pltpu.make_async_copy(roww_hbm, roww, load_sem.at[2]),
+        pltpu.make_async_copy(colw_hbm, colw, load_sem.at[3]),
+    ]
 
     numbers = [
-        pltpu.make_async_copy(srow_hbm, srow_ref, ask_local.at[1]),
-        pltpu.make_async_copy(ask_hbm, sblock_ref, ask_local.at[2]),
+        pltpu.make_async_copy(srow_hbm, srow_ref, ask_local.at[0]),
+        pltpu.make_async_copy(ask_hbm, sblock_ref, ask_local.at[1]),
     ]
     for copy in numbers:
         copy.start()
@@ -149,11 +161,6 @@
         remote(padded.at[every_r, inner_west], padded.at[every_r, east], halo_send.at[2], halo_recv.at[2], (row, left)),
         remote(padded.at[every_r, inner_east], padded.at[every_r, west], halo_send.at[3], halo_recv.at[3], (row, right)),
     ]
-    load_roww = pltpu.make_async_copy(roww_hbm, roww, load_sem.at[TC_DEV])
-    load_colw = pltpu.make_async_copy(colw_hbm, colw, load_sem.at[TC_DEV + 1])
-    load_roww.start()
-    load_colw.start()
-
     def clear(where):
         shape = tuple(s.size for s in where)
         padded[where] = jnp.zeros(shape, jnp.float32)
@@ -175,16 +182,30 @@
         for copy in numbers:
             copy.wait()
 
-    arrived = set()
-
     pool = pooling_matrix()
+    bands = rows // BAND
+    per_piece = B // BAND
+    units = [(step, ORDER[step], half * HALF, HALF) for step in range(2) for half in range(2)]
+    units += [(step, m, 0, B) for step, m in enumerate(ORDER) if step > 1]
+    half_bands = HALF // BAND
+    ahead = 3
+
+    def half_band(i, half):
+        return lax.div(i, half_bands) * per_piece + lax.rem(i, half_bands) + half * half_bands
+
+    blind = []
+
+    def send_blind(k):
+        for side, (device, place) in enumerate((((up, col), 1), ((down, col), 0))):
+            copy = remote(
+                blind_send.at[k], blind_got.at[place, k], blind_sems.at[0, side, k], blind_sems.at[1, side, k], device
+            )
+            copy.start()
+            blind.append(copy)
+
     strips = []
-    for step, m in enumerate(ORDER):
-        if step == 2:
-            for k in (0, last):
-                if k not in arrived:
-                    loads[k].wait()
-                    arrived.add(k)
+    for unit, (step, m, offset, height) in enumerate(units):
+        if unit == 4:
             for copy in sides:
                 copy.start()
         if step == 4:
@@ -208,43 +229,66 @@
             shaded[slot, pl.ds(start, BAND), :] = shade(cells, BAND).astype(jnp.bfloat16)
             return carry
 
-        for k in (m - 1, m, m + 1):
-            if 0 <= k <= last and k not in arrived:
-                loads[k].wait()
-                arrived.add(k)
-        bands = rows // BAND
-        if step == 0:
-            lax.fori_loop(1, bands - 1, shade_band, 0, unroll=2)
+        def first_half(i, carry, shade_band=shade_band):
+            return shade_band(half_band(i, 0), carry)
+
+        def second_half(i, carry, shade_band=shade_band):
+            return shade_band(half_band(i, 1), carry)
+
+        sent = slice(offset, offset + height)
+        if unit == 0:
+            for k in range(pieces):
+                first_load(k).wait()
+                shade_band(k * per_piece + 1, 0)
+                rows_k = slice(k * B + BAND, k * B + 2 * BAND)
+                blind_send[k] = shaded[slot, rows_k, :]
+                if k > 0:
+                    send_blind(k - 1)
+            for copy in rest:
+                copy.start()
+            lax.fori_loop(1, pieces, lambda k, c: shade_band(k * per_piece, c), 0)
+            send_blind(pieces - 1)
+            lax.fori_loop(0, ahead, second_half, 0)
             first_halo()
-            lax.fori_loop(0, 2, lambda i, c: shade_band(i * (bands - 1), c), 0)
+            shade_band(0, 0)
+            sent = slice(0, BAND)
+        elif unit == 1:
+            lax.fori_loop(ahead, pieces * half_bands, second_half, 0)
+        elif unit == 2:
+            rest[0].wait()
+            rest[1].wait()
+            lax.fori_loop(0, pieces * half_bands, first_half, 0, unroll=2)
+        elif unit == 3:
+            lax.fori_loop(0, pieces * half_bands, second_half, 0, unroll=2)
         else:
             lax.fori_loop(0, bands, shade_band, 0, unroll=2)
+        part = slice(offset, offset + height)
+        blocks = [slice(k * B + offset, k * B + offset + height) for k in range(pieces)]
+        asked_rows = [slice(k * B + sent.start, k * B + sent.stop) for k in range(pieces)]
         for g in range(TR_DEV):
             for side in range(2):
-                sendbuf[side, m, g] = chosen(
-                    lax.div(asked_s[side, 0, g * TC_DEV], TC_DEV),
-                    [shaded[slot, k * B : (k + 1) * B, :] for k in range(rows // B)],
+                sendbuf[side, m, g, sent, :] = chosen(
+                    lax.div(asked_s[side, 0, g * TC_DEV], TC_DEV), [shaded[slot, k, :] for k in asked_rows]
                 )
         for g in range(TR_DEV):
             for side, (device, place) in enumerate((((up, col), 2), ((down, col), 0))):
+                sems = (strip_send.at[side, m, g], strip_recv.at[side, m, g])
+                if step < 2 and offset == 0:
+                    sems = (early_send.at[side, step, g], early_recv.at[side, step, g])
                 copy = remote(
-                    sendbuf.at[side, m, g],
-                    recv[m * TR_DEV + g].at[place],
-                    strip_send.at[side, m, g],
-                    strip_recv.at[side, m, g],
+                    sendbuf.at[side, m, g, sent, :],
+                    recv[m * TR_DEV + g].at[place, sent, :],
+                    *sems,
                     device,
                 )
                 copy.start()
-                strips.append(((step, g, side), copy))
+                strips.append(((step, g), copy))
         for g in range(TR_DEV):
-            recv[(last - m) * TR_DEV + g][1] = chosen(
-                lax.div(sblock_ref[0, g * TC_DEV], TC_DEV),
-                [shaded[slot, k * B : (k + 1) * B, :] for k in range(rows // B)],
+            recv[(last - m) * TR_DEV + g][1, part, :] = chosen(
+                lax.div(sblock_ref[0, g * TC_DEV], TC_DEV), [shaded[slot, k, :] for k in blocks]
             )
-    strips = dict(strips)
-
-    load_roww.wait()
-    load_colw.wait()
+    rest[2].wait()
+    rest[3].wait()
     outs = []
     two_copy = remote(two_send, two_got, two_sems.at[0], two_sems.at[1], (row + 1 - 2 * parity, col))
 
@@ -297,10 +341,22 @@
     done = set()
     for step, m in enumerate(ORDER):
         for g in range(TR_DEV):
-            strips[step, g, 0].wait_recv()
-            strips[step, g, 1].wait_recv()
+            for key, copy in strips:
+                if key == (step, g):
+                    copy.wait_recv()
             side = srow_ref[0, g * TC_DEV] - row + 1
-            merged[g, m] = chosen(side, [recv[m * TR_DEV + g][k] for k in range(3)])
+            if step == 0:
+                if g == 0:
+                    for copy in blind:
+                        copy.wait_recv()
+                block = lax.div(sblock_ref[0, g * TC_DEV], TC_DEV)
+                rows_b = slice(BAND, 2 * BAND)
+                from_up, from_down = (chosen(block, [blind_got[p, k] for k in range(pieces)]) for p in range(2))
+                merged[g, m, rows_b, :] = chosen(side, [from_up, recv[m * TR_DEV + g][1, rows_b, :], from_down])
+                for rows_b in (slice(0, BAND), slice(2 * BAND, B)):
+                    merged[g, m, rows_b, :] = chosen(side, [recv[m * TR_DEV + g][k, rows_b, :] for k in range(3)])
+            else:
+                merged[g, m] = chosen(side, [recv[m * TR_DEV + g][k] for k in range(3)])
             for target in READY[step]:
                 make_target(g, target)
                 done.add((g, target))
@@ -315,7 +371,7 @@
     for copy in outs:
         copy.wait()
     two_copy.wait_send()
-    for copy in asks + halos + sides + list(strips.values()):
+    for copy in asks + halos + sides + blind + [copy for _, copy in strips]:
         copy.wait_send()
 
 
@@ -405,10 +461,13 @@
             vmem((HALF, B), f32),
             vmem((HALF, B), bf16),
             vmem((len(LATE), B, B), bf16),
+            vmem((rows // B, BAND, B), bf16),
+            vmem((2, rows // B, BAND, B), bf16),
         ]
         + [vmem((3, B, B), bf16)] * targets
         + [
-            dma((TC_DEV + 2,)), dma((2,)), dma((2,)), dma((3,)), dma((4,)), dma((4,)),
+            dma((rows // B,)), dma((4,)), dma((2, 2, TR_DEV)), dma((2, 2, TR_DEV)),
+            dma((2, 2, rows // B)), dma((2,)), dma((2,)), dma((2,)), dma((4,)), dma((4,)),
             dma((2, TC_DEV, TR_DEV)), dma((2, TC_DEV, TR_DEV)), dma((2,)), dma((n_out,)),
         ],
         compiler_params=pltpu.CompilerParams(

time: 63.7 us -> 62.8 us (0.986)
  Pallas kernels: 62.9 us -> 62.1 us
    pallas_call x1, Pallas kernels: 60.4 us -> 59.5 us  [per_device(): pl.pallas_call(functools.partial(kernel, n_row, n_col), out_shape=(*image...]
where the time goes in v4:
time: 62.8 us; the launch traced here: 62.7 us
  Pallas kernels  62.1 us (99%)
  between operations  0.64 us (1%)
    pallas_call x1, Pallas kernels, per_device(): pl.pallas_call(functools.partial(kernel, n_row, n_col), out_shape=(*image...  59.5 us
    pallas_call x1, Pallas kernels, per_device(): pl.pallas_call(finish, out_shape=images, in_specs=[anywhere] * 3 + [pl.Bl...  2.53 us

profile of v4, /device:TPU:0, one launch (start us, length us, event | category | flops | bytes accessed | tf_op | source)
XLA Modules:
  0.0 62.7 jit_solution(14242375092001830060)
XLA Ops:
  0.6 59.5 %hillshade_tiles.1 = (f32[512,2048]{1,0:T(8,128)S(1)}, f32[256,1024]{1,0:T(8,128)S(1)}, f32[128,256]{1,0:T(8,128)S(1)}, bf16[128,256]{1,0:T(8,128)(2,1)S(1)}, bf16[3,2,256,256]{3,2,1,0:T(8,128)(2,1)S(1)}) custom-call(s32[1,16]{1,0:T(1,128)} %bitcast.3, s32[1,16]{1,0:T(1,128)} %bitcast.4, f32[1024,2048]{1,0:T(8,128)} %elev_hbm.1, ...), custom_call_target="tpu_custom_call" | custom-call | tf_op jit(solution)/shard_map/hillshade_tiles/pallas_call | solution.py:439
  60.2 2.5 %hillshade_finish.1 = (f32[512,2048]{1,0:T(8,128)}, f32[256,1024]{1,0:T(8,128)}, f32[256,256]{1,0:T(8,128)}) custom-call(f32[512,2048]{1,0:T(8,128)S(1)} %get-tuple-element.11.merc_in, f32[256,1024]{1,0:T(8,128)S(1)} %get-tuple-element.12.one_in, f32[128,256]{1,0:T(8,128)S(1)} %get-tuple-element.13.two_in, bf16[128,256]{1,0:T(8,128)(2,1)S(1)} %get-tuple-element.14.two_got, ...), custom_call_target="tpu_custom_call" | custom-call | tf_op jit(solution)/shard_map/hillshade_finish/pallas_call | solution.py:478

commit v5 on v4

--- a/solution.py
+++ b/solution.py
@@ -130,6 +130,8 @@
     barrier = pltpu.get_barrier_semaphore()
     for device in around:
         pl.semaphore_signal(barrier, inc=1, device_id=device, device_id_type=MESH)
+    for copy in numbers:
+        copy.wait()
     pl.semaphore_wait(barrier, len(around))
 
     def remote(src, dst, send_sem, recv_sem, device):
@@ -138,8 +140,8 @@
         )
 
     asks = [
-        remote(ask_hbm, asked_s.at[1], ask_send.at[0], ask_recv.at[1], (up, col)),
-        remote(ask_hbm, asked_s.at[0], ask_send.at[1], ask_recv.at[0], (down, col)),
+        remote(sblock_ref, asked_s.at[1], ask_send.at[0], ask_recv.at[1], (up, col)),
+        remote(sblock_ref, asked_s.at[0], ask_send.at[1], ask_recv.at[0], (down, col)),
     ]
     for copy in asks:
         copy.start()
@@ -179,16 +181,13 @@
         def _():
             clear((bottom, mid_c))
 
-        for copy in numbers:
-            copy.wait()
-
     pool = pooling_matrix()
     bands = rows // BAND
     per_piece = B // BAND
     units = [(step, ORDER[step], half * HALF, HALF) for step in range(2) for half in range(2)]
     units += [(step, m, 0, B) for step, m in enumerate(ORDER) if step > 1]
     half_bands = HALF // BAND
-    ahead = 3
+    ahead = 6
 
     def half_band(i, half):
         return lax.div(i, half_bands) * per_piece + lax.rem(i, half_bands) + half * half_bands

time: 62.8 us -> 62.3 us (level)
  no operation moved by 1% of the time
where the time goes in v5:
time: 62.3 us; the launch traced here: 62.2 us
  Pallas kernels  61.5 us (99%)
  between operations  0.64 us (1%)
    pallas_call x1, Pallas kernels, per_device(): pl.pallas_call(functools.partial(kernel, n_row, n_col), out_shape=(*image...  59 us
    pallas_call x1, Pallas kernels, per_device(): pl.pallas_call(finish, out_shape=images, in_specs=[anywhere] * 3 + [pl.Bl...  2.53 us

profile of v5, /device:TPU:0, one launch (start us, length us, event | category | flops | bytes accessed | tf_op | source)
XLA Modules:
  0.0 62.2 jit_solution(9233000450163569564)
XLA Ops:
  0.6 59.0 %hillshade_tiles.1 = (f32[512,2048]{1,0:T(8,128)S(1)}, f32[256,1024]{1,0:T(8,128)S(1)}, f32[128,256]{1,0:T(8,128)S(1)}, bf16[128,256]{1,0:T(8,128)(2,1)S(1)}, bf16[3,2,256,256]{3,2,1,0:T(8,128)(2,1)S(1)}) custom-call(s32[1,16]{1,0:T(1,128)} %bitcast.3, s32[1,16]{1,0:T(1,128)} %bitcast.4, f32[1024,2048]{1,0:T(8,128)} %elev_hbm.1, ...), custom_call_target="tpu_custom_call" | custom-call | tf_op jit(solution)/shard_map/hillshade_tiles/pallas_call | solution.py:438
  59.6 2.5 %hillshade_finish.1 = (f32[512,2048]{1,0:T(8,128)}, f32[256,1024]{1,0:T(8,128)}, f32[256,256]{1,0:T(8,128)}) custom-call(f32[512,2048]{1,0:T(8,128)S(1)} %get-tuple-element.11.merc_in, f32[256,1024]{1,0:T(8,128)S(1)} %get-tuple-element.12.one_in, f32[128,256]{1,0:T(8,128)S(1)} %get-tuple-element.13.two_in, bf16[128,256]{1,0:T(8,128)(2,1)S(1)} %get-tuple-element.14.two_got, ...), custom_call_target="tpu_custom_call" | custom-call | tf_op jit(solution)/shard_map/hillshade_finish/pallas_call | solution.py:477

commit v6 on v5

--- a/solution.py
+++ b/solution.py
@@ -149,11 +149,13 @@
     top, bottom = pl.ds(0, PAD_R), pl.ds(PAD_R + rows, PAD_R)
     mid_c = pl.ds(PAD_C, cols)
     west, east = pl.ds(0, PAD_C), pl.ds(PAD_C + cols, PAD_C)
-    first_r, last_r = pl.ds(0, PAD_R), pl.ds(rows - PAD_R, PAD_R)
     all_c = pl.ds(0, cols)
+    edge_top, edge_bottom = pl.ds(PAD_R - 1, 1), pl.ds(PAD_R + rows, 1)
     halos = [
-        remote(elev_hbm.at[first_r, all_c], padded.at[bottom, mid_c], halo_send.at[0], halo_recv.at[0], (up, col)),
-        remote(elev_hbm.at[last_r, all_c], padded.at[top, mid_c], halo_send.at[1], halo_recv.at[1], (down, col)),
+        remote(elev_hbm.at[pl.ds(0, 1), all_c], padded.at[edge_bottom, mid_c], halo_send.at[0], halo_recv.at[0], (up, col)),
+        remote(
+            elev_hbm.at[pl.ds(rows - 1, 1), all_c], padded.at[edge_top, mid_c], halo_send.at[1], halo_recv.at[1], (down, col)
+        ),
     ]
     for copy in halos:
         copy.start()

time: 62.3 us -> 61.7 us (level)
  no operation moved by 1% of the time
where the time goes in v6:
time: 61.7 us; the launch traced here: 61.5 us
  Pallas kernels  60.9 us (99%)
  between operations  0.64 us (1%)
    pallas_call x1, Pallas kernels, per_device(): pl.pallas_call(functools.partial(kernel, n_row, n_col), out_shape=(*image...  58.4 us
    pallas_call x1, Pallas kernels, per_device(): pl.pallas_call(finish, out_shape=images, in_specs=[anywhere] * 3 + [pl.Bl...  2.53 us

profile of v6, /device:TPU:0, one launch (start us, length us, event | category | flops | bytes accessed | tf_op | source)
XLA Modules:
  0.0 61.5 jit_solution(11604461293326310505)
XLA Ops:
  0.6 58.4 %hillshade_tiles.1 = (f32[512,2048]{1,0:T(8,128)S(1)}, f32[256,1024]{1,0:T(8,128)S(1)}, f32[128,256]{1,0:T(8,128)S(1)}, bf16[128,256]{1,0:T(8,128)(2,1)S(1)}, bf16[3,2,256,256]{3,2,1,0:T(8,128)(2,1)S(1)}) custom-call(s32[1,16]{1,0:T(1,128)} %bitcast.3, s32[1,16]{1,0:T(1,128)} %bitcast.4, f32[1024,2048]{1,0:T(8,128)} %elev_hbm.1, ...), custom_call_target="tpu_custom_call" | custom-call | tf_op jit(solution)/shard_map/hillshade_tiles/pallas_call | solution.py:440
  59.0 2.5 %hillshade_finish.1 = (f32[512,2048]{1,0:T(8,128)}, f32[256,1024]{1,0:T(8,128)}, f32[256,256]{1,0:T(8,128)}) custom-call(f32[512,2048]{1,0:T(8,128)S(1)} %get-tuple-element.11.merc_in, f32[256,1024]{1,0:T(8,128)S(1)} %get-tuple-element.12.one_in, f32[128,256]{1,0:T(8,128)S(1)} %get-tuple-element.13.two_in, bf16[128,256]{1,0:T(8,128)(2,1)S(1)} %get-tuple-element.14.two_got, ...), custom_call_target="tpu_custom_call" | custom-call | tf_op jit(solution)/shard_map/hillshade_finish/pallas_call | solution.py:479

commit v7 on v6

--- a/solution.py
+++ b/solution.py
@@ -95,6 +95,18 @@
     def sent_col(m):
         return m + parity * (last - 2 * m)
 
+    numbers = [
+        pltpu.make_async_copy(srow_hbm, srow_ref, ask_local.at[0]),
+        pltpu.make_async_copy(ask_hbm, sblock_ref, ask_local.at[1]),
+    ]
+    for copy in numbers:
+        copy.start()
+
+    around = [(up, col), (down, col), (row, left), (row, right)]
+    barrier = pltpu.get_barrier_semaphore()
+    for device in around:
+        pl.semaphore_signal(barrier, inc=1, device_id=device, device_id_type=MESH)
+
     pieces = rows // B
     span = B + 2 * PAD_C
     first_lane = pl.multiple_of(sent_col(ORDER[0]) * B - PAD_C, PAD_C)
@@ -119,17 +131,6 @@
         pltpu.make_async_copy(colw_hbm, colw, load_sem.at[3]),
     ]
 
-    numbers = [
-        pltpu.make_async_copy(srow_hbm, srow_ref, ask_local.at[0]),
-        pltpu.make_async_copy(ask_hbm, sblock_ref, ask_local.at[1]),
-    ]
-    for copy in numbers:
-        copy.start()
-
-    around = [(up, col), (down, col), (row, left), (row, right)]
-    barrier = pltpu.get_barrier_semaphore()
-    for device in around:
-        pl.semaphore_signal(barrier, inc=1, device_id=device, device_id_type=MESH)
     for copy in numbers:
         copy.wait()
     pl.semaphore_wait(barrier, len(around))

time: 61.7 us -> 61.6 us (level)
  no operation moved by 1% of the time
where the time goes in v7:
time: 61.6 us; the launch traced here: 61.5 us
  Pallas kernels  60.9 us (99%)
  between operations  0.64 us (1%)
    pallas_call x1, Pallas kernels, per_device(): pl.pallas_call(functools.partial(kernel, n_row, n_col), out_shape=(*image...  58.4 us
    pallas_call x1, Pallas kernels, per_device(): pl.pallas_call(finish, out_shape=images, in_specs=[anywhere] * 3 + [pl.Bl...  2.53 us

profile of v7, /device:TPU:0, one launch (start us, length us, event | category | flops | bytes accessed | tf_op | source)
XLA Modules:
  0.0 61.5 jit_solution(11997331160993103539)
XLA Ops:
  0.6 58.4 %hillshade_tiles.1 = (f32[512,2048]{1,0:T(8,128)S(1)}, f32[256,1024]{1,0:T(8,128)S(1)}, f32[128,256]{1,0:T(8,128)S(1)}, bf16[128,256]{1,0:T(8,128)(2,1)S(1)}, bf16[3,2,256,256]{3,2,1,0:T(8,128)(2,1)S(1)}) custom-call(s32[1,16]{1,0:T(1,128)} %bitcast.3, s32[1,16]{1,0:T(1,128)} %bitcast.4, f32[1024,2048]{1,0:T(8,128)} %elev_hbm.1, ...), custom_call_target="tpu_custom_call" | custom-call | tf_op jit(solution)/shard_map/hillshade_tiles/pallas_call | solution.py:441
  59.0 2.5 %hillshade_finish.1 = (f32[512,2048]{1,0:T(8,128)}, f32[256,1024]{1,0:T(8,128)}, f32[256,256]{1,0:T(8,128)}) custom-call(f32[512,2048]{1,0:T(8,128)S(1)} %get-tuple-element.11.merc_in, f32[256,1024]{1,0:T(8,128)S(1)} %get-tuple-element.12.one_in, f32[128,256]{1,0:T(8,128)S(1)} %get-tuple-element.13.two_in, bf16[128,256]{1,0:T(8,128)(2,1)S(1)} %get-tuple-element.14.two_got, ...), custom_call_target="tpu_custom_call" | custom-call | tf_op jit(solution)/shard_map/hillshade_finish/pallas_call | solution.py:480
